TPU v7x, 32 devices: a whole 2x2x4 slice. The times are simulated.
32 devices in a mesh: ctx: 8 (over z, y), dp: 4 (over x, core).
Axes of the slice: x: 2, y: 2, z: 4, core: 2. Of those that a mesh axis runs over, the one named last changes fastest.
Arguments:
- tokens: bfloat16 [4, 4096, 768], P('dp', 'ctx'), may hold values from -6 to 6
- cotangent: bfloat16 [4, 4096, 768], P('dp', 'ctx'), may hold values from -6 to 6
- attn_gain: bfloat16 [768], P('dp'), may hold values from 0.099609375 to 1.8984375
- mlp_gain: bfloat16 [768], P('dp'), may hold values from 0.099609375 to 1.8984375
- w_qkv: bfloat16 [768, 2304], P('dp'), may hold values from -0.21875 to 0.21875
- w_out: bfloat16 [768, 768], P('dp'), may hold values from -6 to 6
- w_in: bfloat16 [768, 2304], P('dp'), may hold values from -0.21875 to 0.21875
- w_mlp_out: bfloat16 [1152, 768], P('dp'), may hold values from -0.1875 to 0.1875
- block_offsets: int32 [4, 8], P('dp', 'ctx'), may hold values from 0 to 3584, as said below
Outputs:
- mixed: bfloat16 [4, 4096, 768], P('dp', 'ctx')
- tokens_grad: float32 [4, 4096, 768], P('dp', 'ctx')
- attn_gain_grad: float32 [768], P('dp')
- mlp_gain_grad: float32 [768], P('dp')
- w_qkv_grad: float32 [768, 2304], P('dp')
- w_out_grad: float32 [768, 768], P('dp')
- w_in_grad: float32 [768, 2304], P('dp')
- w_mlp_out_grad: float32 [1152, 768], P('dp')
Inputs may be any that keep to these rules, and one draw needn't show every extreme that they name: `block_offsets`: each row holds every multiple of 512 below 4096 exactly once.
All inputs are finite; a program needn't handle non-finite values.
Results may differ from a plain program's by a relative error of at most 0.022.
Values may be sent and summed in bfloat16 or wider, within the bound.
No kernel may reach another device: no remote copies, remote signals or barrier semaphores. Data moves between devices by JAX's collectives and lax.ppermute only.
A program may use at most 128 MiB of HBM per device.

v0:
```python
import jax
import jax.numpy as jnp
from jax import lax
from jax.sharding import PartitionSpec as P

HEADS = 12
HEAD_DIM = 64
FF = 1152
rope_base = 160000.0
norm_eps = 1e-05


def passed_along(x, axis, by):
    count = lax.axis_size(axis)
    return lax.ppermute(x, axis, [(i, (i + by) % count) for i in range(count)])


def layer_norm(values, gain):
    center = values - jnp.mean(values, axis=-1, keepdims=True)
    spread = jnp.mean(center * center, axis=-1, keepdims=True)
    return center * lax.rsqrt(spread + norm_eps) * gain


def norm_back(values, gain, upstream):
    _, pull = jax.vjp(layer_norm, values, gain)
    return pull(upstream)


def rotary_tables(positions, half_size):
    frequency = rope_base ** (-jnp.arange(half_size, dtype=jnp.float32) / half_size)
    angles = positions[:, None] * frequency[None, :]
    cosine = jnp.cos(angles)
    sine_table = jnp.sin(angles)
    return (jnp.concatenate([cosine, cosine], -1), jnp.concatenate([sine_table, sine_table], -1))


def rotate(values, cosine, sine_table):
    half_size = values.shape[-1] // 2
    turned = jnp.concatenate([-values[..., half_size:], values[..., :half_size]], -1)
    return values * cosine[:, None, :] + turned * sine_table[:, None, :]


def unrotate(upstream, cosine, sine_table):
    half_size = upstream.shape[-1] // 2
    turned = upstream * sine_table[:, None, :]
    return upstream * cosine[:, None, :] + jnp.concatenate(
        [turned[..., half_size:], -turned[..., :half_size]], -1
    )


def geglu(packed, hidden_size):
    return jax.nn.gelu(packed[:, :hidden_size], approximate=False) * packed[:, hidden_size:]


def product(left, right):
    return jnp.dot(left, right, preferred_element_type=jnp.float32)


def transposed_left(left, right):
    return lax.dot_general(
        left, right, (((0,), (0,)), ((), ())), preferred_element_type=jnp.float32
    )


def transposed_right(left, right):
    return lax.dot_general(
        left, right, (((1,), (1,)), ((), ())), preferred_element_type=jnp.float32
    )


def key_block():
    return 512


def body(tokens, cotangent, attn_gain, mlp_gain, w_qkv, w_out, w_in, w_mlp_out, block_offsets):
    head_count = HEADS
    head_size = HEAD_DIM
    hidden_size = FF
    model_width = head_count * head_size
    scale = head_size ** (-0.5)
    inputs = tokens[0].astype(jnp.float32)
    row_count = inputs.shape[0]
    positions = (block_offsets[0, 0] + jnp.arange(row_count, dtype=jnp.int32)).astype(jnp.float32)
    cosine, sine_table = rotary_tables(positions, head_size // 2)
    gain_one, gain_two, weight_qkv, weight_out, weight_in, weight_down = (
        lax.all_gather(attn_gain, "dp", axis=0, tiled=True),
        lax.all_gather(mlp_gain, "dp", axis=0, tiled=True),
        lax.all_gather(w_qkv, "dp", axis=0, tiled=True),
        lax.all_gather(w_out, "dp", axis=0, tiled=True),
        lax.all_gather(w_in, "dp", axis=0, tiled=True),
        lax.all_gather(w_mlp_out, "dp", axis=0, tiled=True),
    )
    first_gain = gain_one.astype(jnp.float32)
    second_gain = gain_two.astype(jnp.float32)
    normed = layer_norm(inputs, first_gain).astype(jnp.bfloat16)
    packed = product(normed, weight_qkv).reshape(row_count, 3, head_count, head_size)
    queries = rotate(packed[:, 0], cosine, sine_table).astype(jnp.bfloat16)
    keys_local = (
        rotate(packed[:, 1], cosine, sine_table)
        .astype(jnp.bfloat16)
        .reshape(row_count, model_width)
    )
    values_local = packed[:, 2].astype(jnp.bfloat16).reshape(row_count, model_width)

    def attend(carried, blocks):
        running_max, running_sum, running_out = carried
        key_part, value_part = blocks
        scores = (
            jnp.einsum("qhd,khd->hqk", queries, key_part, preferred_element_type=jnp.float32)
            * scale
        )
        new_max = jnp.maximum(running_max, jnp.max(scores, axis=-1))
        rescale = jnp.exp(running_max - new_max)
        weights = jnp.exp(scores - new_max[:, :, None])
        running_sum = running_sum * rescale + jnp.sum(weights, axis=-1)
        running_out = running_out * rescale.T[:, :, None] + jnp.einsum(
            "hqk,khd->qhd",
            weights.astype(jnp.bfloat16),
            value_part,
            preferred_element_type=jnp.float32,
        )
        return ((new_max, running_sum, running_out), None)

    initial = (
        jnp.full((head_count, row_count), -1e30, jnp.float32),
        jnp.zeros((head_count, row_count), jnp.float32),
        jnp.zeros((row_count, head_count, head_size), jnp.float32),
    )
    carried = initial
    shards = (
        lax.all_gather(keys_local, "ctx", axis=0, tiled=True),
        lax.all_gather(values_local, "ctx", axis=0, tiled=True),
    )
    key_count = shards[0].shape[0]
    block_size = key_block()
    split_keys = shards[0].reshape(key_count // block_size, block_size, head_count, head_size)
    split_values = shards[1].reshape(key_count // block_size, block_size, head_count, head_size)
    carried, _ = lax.scan(attend, carried, (split_keys, split_values))
    running_max, running_sum, running_out = carried
    attended = running_out / running_sum.T[:, :, None]
    log_total = running_max + jnp.log(running_sum)
    attended_low = attended.reshape(row_count, model_width).astype(jnp.bfloat16)
    residual = inputs + product(attended_low, weight_out)
    mlp_normed = layer_norm(residual, second_gain).astype(jnp.bfloat16)
    up_gate = product(mlp_normed, weight_in)
    joined = geglu(up_gate, hidden_size).astype(jnp.bfloat16)
    outputs = residual + product(joined, weight_down)
    mixed = outputs.astype(jnp.bfloat16)[None]
    gain_one, gain_two, weight_qkv, weight_out, weight_in, weight_down = (
        lax.all_gather(attn_gain, "dp", axis=0, tiled=True),
        lax.all_gather(mlp_gain, "dp", axis=0, tiled=True),
        lax.all_gather(w_qkv, "dp", axis=0, tiled=True),
        lax.all_gather(w_out, "dp", axis=0, tiled=True),
        lax.all_gather(w_in, "dp", axis=0, tiled=True),
        lax.all_gather(w_mlp_out, "dp", axis=0, tiled=True),
    )
    first_gain = gain_one.astype(jnp.float32)
    second_gain = gain_two.astype(jnp.float32)
    upstream = cotangent[0].astype(jnp.float32)
    upstream_low = upstream.astype(jnp.bfloat16)
    grad_down = transposed_left(joined, upstream_low)
    grad_joined = transposed_right(upstream_low, weight_down)
    _, glu_pull = jax.vjp(lambda packed_in: geglu(packed_in, hidden_size), up_gate)
    grad_up_gate = glu_pull(grad_joined)[0].astype(jnp.bfloat16)
    grad_in = transposed_left(mlp_normed, grad_up_gate)
    grad_mlp_normed = transposed_right(grad_up_gate, weight_in)
    grad_residual_norm, grad_gain_two = norm_back(residual, second_gain, grad_mlp_normed)
    grad_residual = upstream + grad_residual_norm
    residual_low = grad_residual.astype(jnp.bfloat16)
    grad_out = transposed_left(attended_low, residual_low)
    grad_attended = (
        transposed_right(residual_low, weight_out)
        .astype(jnp.bfloat16)
        .reshape(row_count, head_count, head_size)
    )
    row_delta = jnp.sum(grad_attended.astype(jnp.float32) * attended, axis=-1).T

    def block_grads(query_rows, grad_rows, log_rows, delta_rows, key_rows, value_rows):
        key_count = key_rows.shape[0]
        query_count = query_rows.shape[0]
        block_size = key_block()
        split_keys = key_rows.reshape(key_count // block_size, block_size, head_count, head_size)
        split_values = value_rows.reshape(
            key_count // block_size, block_size, head_count, head_size
        )

        def backward_block(query_grad, blocks):
            key_part, value_part = blocks
            scores = (
                jnp.einsum("qhd,khd->hqk", query_rows, key_part, preferred_element_type=jnp.float32)
                * scale
            )
            probs = jnp.exp(scores - log_rows[:, :, None])
            prob_grad = jnp.einsum(
                "qhd,khd->hqk", grad_rows, value_part, preferred_element_type=jnp.float32
            )
            score_grad = (probs * (prob_grad - delta_rows[:, :, None])).astype(jnp.bfloat16)
            value_grad = jnp.einsum(
                "hqk,qhd->khd",
                probs.astype(jnp.bfloat16),
                grad_rows,
                preferred_element_type=jnp.float32,
            )
            key_grad = (
                jnp.einsum(
                    "hqk,qhd->khd", score_grad, query_rows, preferred_element_type=jnp.float32
                )
                * scale
            )
            query_grad = (
                query_grad
                + jnp.einsum(
                    "hqk,khd->qhd", score_grad, key_part, preferred_element_type=jnp.float32
                )
                * scale
            )
            return (
                query_grad,
                (
                    key_grad.reshape(block_size, model_width),
                    value_grad.reshape(block_size, model_width),
                ),
            )

        query_start = jnp.zeros((query_count, head_count, head_size), jnp.float32)
        query_grad, (key_grad, value_grad) = lax.scan(
            backward_block, query_start, (split_keys, split_values)
        )
        return (
            query_grad,
            key_grad.reshape(key_count, model_width),
            value_grad.reshape(key_count, model_width),
        )

    zero_rows = jnp.zeros((row_count, model_width), jnp.float32)
    zero_heads = jnp.zeros((row_count, head_count, head_size), jnp.float32)

    def cycle_turn(turn_index, carried):
        key_rows, value_rows, key_sum, value_sum, query_sum = carried
        query_add, key_add, value_add = block_grads(
            queries, grad_attended, log_total, row_delta, key_rows, value_rows
        )
        key_sum = key_sum + key_add
        value_sum = value_sum + value_add
        key_rows, value_rows = passed_along((key_rows, value_rows), "ctx", 1)
        key_sum, value_sum = (
            passed_along(key_sum.astype(jnp.bfloat16), "ctx", 1).astype(key_sum.dtype),
            passed_along(value_sum.astype(jnp.bfloat16), "ctx", 1).astype(value_sum.dtype),
        )
        return (key_rows, value_rows, key_sum, value_sum, query_sum + query_add)

    start_state = (keys_local, values_local, zero_rows, zero_rows, zero_heads)
    _, _, grad_keys, grad_values, grad_queries = lax.fori_loop(
        0, lax.axis_size("ctx"), cycle_turn, start_state
    )
    query_back = unrotate(grad_queries, cosine, sine_table).reshape(row_count, model_width)
    key_back = unrotate(
        grad_keys.reshape(row_count, head_count, head_size), cosine, sine_table
    ).reshape(row_count, model_width)
    grad_packed = jnp.concatenate([query_back, key_back, grad_values], axis=1).astype(jnp.bfloat16)
    grad_qkv = transposed_left(normed, grad_packed)
    grad_normed = transposed_right(grad_packed, weight_qkv)
    grad_inputs_norm, grad_gain_one = norm_back(inputs, first_gain, grad_normed)
    tokens_grad = (grad_residual + grad_inputs_norm)[None]
    summed = (
        lax.psum_scatter(
            grad_gain_one.astype(jnp.bfloat16), "dp", scatter_dimension=0, tiled=True
        ).astype(jnp.float32),
        lax.psum_scatter(
            grad_gain_two.astype(jnp.bfloat16), "dp", scatter_dimension=0, tiled=True
        ).astype(jnp.float32),
        lax.psum_scatter(
            grad_qkv.astype(jnp.bfloat16), "dp", scatter_dimension=0, tiled=True
        ).astype(jnp.float32),
        lax.psum_scatter(
            grad_out.astype(jnp.bfloat16), "dp", scatter_dimension=0, tiled=True
        ).astype(jnp.float32),
        lax.psum_scatter(
            grad_in.astype(jnp.bfloat16), "dp", scatter_dimension=0, tiled=True
        ).astype(jnp.float32),
        lax.psum_scatter(
            grad_down.astype(jnp.bfloat16), "dp", scatter_dimension=0, tiled=True
        ).astype(jnp.float32),
    )
    totals = (
        lax.psum(summed[0].astype(jnp.bfloat16), "ctx").astype(jnp.float32),
        lax.psum(summed[1].astype(jnp.bfloat16), "ctx").astype(jnp.float32),
        lax.psum(summed[2].astype(jnp.bfloat16), "ctx").astype(jnp.float32),
        lax.psum(summed[3].astype(jnp.bfloat16), "ctx").astype(jnp.float32),
        lax.psum(summed[4].astype(jnp.bfloat16), "ctx").astype(jnp.float32),
        lax.psum(summed[5].astype(jnp.bfloat16), "ctx").astype(jnp.float32),
    )
    return (mixed, tokens_grad, totals[0], totals[1], totals[2], totals[3], totals[4], totals[5])


def solution(mesh):
    return jax.shard_map(
        body,
        mesh=mesh,
        in_specs=(
            P("dp", "ctx", None),
            P("dp", "ctx", None),
            P("dp"),
            P("dp"),
            P("dp", None),
            P("dp", None),
            P("dp", None),
            P("dp", None),
            P("dp", "ctx"),
        ),
        out_specs=(
            P("dp", "ctx", None),
            P("dp", "ctx", None),
            P("dp"),
            P("dp"),
            P("dp", None),
            P("dp", None),
            P("dp", None),
            P("dp", None),
        ),
        check_vma=False,
    )
```

profile of v0, /device:TPU:0, one launch (start us, length us, event | category | flops | bytes accessed | tf_op | source)
XLA Modules:
  0.0 1304.9 jit_solution(13983983818318694424)
XLA Ops:
  11.6 8.3 all-reduce.9
  21.6 21.4 %all-gather.7.cloned.1.call-done = bf16[768,2304]{1,0:T(8,128)(2,1)} async-done(((bf16[192,2304]{1,0:T(8,128)(2,1)}), bf16[768,2304]{1,0:T(8,128)(2,1)}) %all-gather.7.cloned.1.call-update) | async-done | bytes 3538960 | tf_op jit(solution)/shard_map/all_gather | solution.py:88
  61.9 95.1 %all-gather.9.cloned.1.call-done = bf16[4096,768]{0,1:T(8,128)(2,1)} async-done(((bf16[512,768]{0,1:T(8,128)(2,1)}), bf16[4096,768]{0,1:T(8,128)(2,1)}) %all-gather.9.cloned.1.call-update) | async-done | bytes 6291472 | tf_op jit(solution)/shard_map/all_gather | solution.py:131
  157.0 7.0 copy.35
  168.8 87.9 %all-gather.11.cloned.1.call-done = bf16[4096,768]{0,1:T(8,128)(2,1)} async-done(((bf16[512,768]{0,1:T(8,128)(2,1)}), bf16[4096,768]{0,1:T(8,128)(2,1)}) %all-gather.11.cloned.1.call-update) | async-done | bytes 6291472 | tf_op jit(solution)/shard_map/all_gather | solution.py:132
  256.7 7.0 copy.36
  268.8 145.5 %while.40 = (s32[]{:T(128)}, f32[12,512]{1,0:T(8,128)S(1)}, f32[12,512]{1,0:T(8,128)S(1)}, f32[512,12,64]{0,2,1:T(8,128)S(1)}, bf16[8,512,12,64]{1,3,2,0:T(8,128...) while((s32[]{:T(128)}, f32[12,512]{1,0:T(8,128)S(1)}, ...), condition=%wide.region_5.6_spmd.clone, body=%wide.region_2.5_spmd.clone.sunk | while | flops 831688704 | bytes 93979776 | solution.py:138
  268.8 7.4 bitcast_reduce_fusion.2
  276.3 6.4 bitcast_add_fusion.6
  288.0 7.4 bitcast_reduce_fusion.2
  295.4 6.4 bitcast_add_fusion.6
  306.1 7.4 bitcast_reduce_fusion.2
  313.5 6.7 bitcast_add_fusion.6
  324.5 7.4 bitcast_reduce_fusion.2
  342.5 7.4 bitcast_reduce_fusion.2
  360.5 7.4 bitcast_reduce_fusion.2
  378.4 7.4 bitcast_reduce_fusion.2
  396.4 7.4 bitcast_reduce_fusion.2
  419.6 6.8 fusion.82
  426.5 8.1 fusion.72
  454.6 6.4 convolution_convert_fusion
  461.1 664.6 %while.41 = (s32[]{:T(128)}, bf16[512,768]{0,1:T(8,128)(2,1)}, bf16[512,768]{0,1:T(8,128)(2,1)}, f32[512,768]{0,1:T(8,128)}, f32[512,768]{0,1:T(8,128)}, /*index...) while((s32[]{:T(128)}, bf16[512,768]{0,1:T(8,128)(2,1)}, ...), condition=%wide.region_12.13_spmd.clone, body=%wide.region_11.12_spmd.clone.sunk | while | flops 2043150336 | bytes 191177200 | solution.py:253
  475.6 6.4 fusion.152
  498.8 15.6 %collective-permute-done.3 = bf16[512,768]{0,1:T(8,128)(2,1)} collective-permute-done((bf16[512,768]{0,1:T(8,128)(2,1)}, bf16[512,768]{0,1:T(8,128)(2,1)}, u32[]{:S(2)}, u32[]{:S(2)}) %collective-permute-start.3) | collective-permute-done | bytes 786464 | tf_op jit(solution)/shard_map/while/body/eval_jaxpr/ppermute | solution.py:15
  516.9 14.3 %collective-permute-done = bf16[512,768]{0,1:T(8,128)(2,1)} collective-permute-done((bf16[512,768]{0,1:T(8,128)(2,1)S(1)}, bf16[512,768]{0,1:T(8,128)(2,1)}, u32[]{:S(2)}, u32[]{:S(2)}) %collective-permute-start) | collective-permute-done | bytes 786464 | tf_op jit(solution)/shard_map/while/body/eval_jaxpr/ppermute | solution.py:15
  531.2 14.9 %collective-permute-done.1 = bf16[512,768]{0,1:T(8,128)(2,1)} collective-permute-done((bf16[512,768]{0,1:T(8,128)(2,1)S(1)}, bf16[512,768]{0,1:T(8,128)(2,1)}, u32[]{:S(2)}, u32[]{:S(2)}) %collective-permute-start.1) | collective-permute-done | bytes 786464 | tf_op jit(solution)/shard_map/while/body/eval_jaxpr/ppermute | solution.py:15
  570.7 6.4 bitcast_add_fusion.7
  577.1 6.5 collective-permute-done.2
  585.0 15.6 %collective-permute-done.3 = bf16[512,768]{0,1:T(8,128)(2,1)} collective-permute-done((bf16[512,768]{0,1:T(8,128)(2,1)}, bf16[512,768]{0,1:T(8,128)(2,1)}, u32[]{:S(2)}, u32[]{:S(2)}) %collective-permute-start.3) | collective-permute-done | bytes 786464 | tf_op jit(solution)/shard_map/while/body/eval_jaxpr/ppermute | solution.py:15
  603.1 14.4 %collective-permute-done = bf16[512,768]{0,1:T(8,128)(2,1)} collective-permute-done((bf16[512,768]{0,1:T(8,128)(2,1)S(1)}, bf16[512,768]{0,1:T(8,128)(2,1)}, u32[]{:S(2)}, u32[]{:S(2)}) %collective-permute-start) | collective-permute-done | bytes 786464 | tf_op jit(solution)/shard_map/while/body/eval_jaxpr/ppermute | solution.py:15
  617.4 14.0 %collective-permute-done.1 = bf16[512,768]{0,1:T(8,128)(2,1)} collective-permute-done((bf16[512,768]{0,1:T(8,128)(2,1)S(1)}, bf16[512,768]{0,1:T(8,128)(2,1)}, u32[]{:S(2)}, u32[]{:S(2)}) %collective-permute-start.1) | collective-permute-done | bytes 786464 | tf_op jit(solution)/shard_map/while/body/eval_jaxpr/ppermute | solution.py:15
  654.2 6.4 bitcast_add_fusion.7
  660.6 8.4 collective-permute-done.2
  670.3 15.6 %collective-permute-done.3 = bf16[512,768]{0,1:T(8,128)(2,1)} collective-permute-done((bf16[512,768]{0,1:T(8,128)(2,1)}, bf16[512,768]{0,1:T(8,128)(2,1)}, u32[]{:S(2)}, u32[]{:S(2)}) %collective-permute-start.3) | collective-permute-done | bytes 786464 | tf_op jit(solution)/shard_map/while/body/eval_jaxpr/ppermute | solution.py:15
  688.4 14.4 %collective-permute-done = bf16[512,768]{0,1:T(8,128)(2,1)} collective-permute-done((bf16[512,768]{0,1:T(8,128)(2,1)S(1)}, bf16[512,768]{0,1:T(8,128)(2,1)}, u32[]{:S(2)}, u32[]{:S(2)}) %collective-permute-start) | collective-permute-done | bytes 786464 | tf_op jit(solution)/shard_map/while/body/eval_jaxpr/ppermute | solution.py:15
  702.8 13.1 %collective-permute-done.1 = bf16[512,768]{0,1:T(8,128)(2,1)} collective-permute-done((bf16[512,768]{0,1:T(8,128)(2,1)S(1)}, bf16[512,768]{0,1:T(8,128)(2,1)}, u32[]{:S(2)}, u32[]{:S(2)}) %collective-permute-start.1) | collective-permute-done | bytes 786464 | tf_op jit(solution)/shard_map/while/body/eval_jaxpr/ppermute | solution.py:15
  737.9 6.4 bitcast_add_fusion.7
  744.3 9.2 collective-permute-done.2
  754.9 15.6 %collective-permute-done.3 = bf16[512,768]{0,1:T(8,128)(2,1)} collective-permute-done((bf16[512,768]{0,1:T(8,128)(2,1)}, bf16[512,768]{0,1:T(8,128)(2,1)}, u32[]{:S(2)}, u32[]{:S(2)}) %collective-permute-start.3) | collective-permute-done | bytes 786464 | tf_op jit(solution)/shard_map/while/body/eval_jaxpr/ppermute | solution.py:15
  772.9 14.4 %collective-permute-done = bf16[512,768]{0,1:T(8,128)(2,1)} collective-permute-done((bf16[512,768]{0,1:T(8,128)(2,1)S(1)}, bf16[512,768]{0,1:T(8,128)(2,1)}, u32[]{:S(2)}, u32[]{:S(2)}) %collective-permute-start) | collective-permute-done | bytes 786464 | tf_op jit(solution)/shard_map/while/body/eval_jaxpr/ppermute | solution.py:15
  787.3 12.3 collective-permute-done.1
  821.4 6.4 bitcast_add_fusion.7
  827.8 9.3 collective-permute-done.2
  838.5 15.6 %collective-permute-done.3 = bf16[512,768]{0,1:T(8,128)(2,1)} collective-permute-done((bf16[512,768]{0,1:T(8,128)(2,1)}, bf16[512,768]{0,1:T(8,128)(2,1)}, u32[]{:S(2)}, u32[]{:S(2)}) %collective-permute-start.3) | collective-permute-done | bytes 786464 | tf_op jit(solution)/shard_map/while/body/eval_jaxpr/ppermute | solution.py:15
  856.6 14.4 %collective-permute-done = bf16[512,768]{0,1:T(8,128)(2,1)} collective-permute-done((bf16[512,768]{0,1:T(8,128)(2,1)S(1)}, bf16[512,768]{0,1:T(8,128)(2,1)}, u32[]{:S(2)}, u32[]{:S(2)}) %collective-permute-start) | collective-permute-done | bytes 786464 | tf_op jit(solution)/shard_map/while/body/eval_jaxpr/ppermute | solution.py:15
  871.0 11.4 collective-permute-done.1
  904.2 6.4 bitcast_add_fusion.7
  910.6 9.3 collective-permute-done.2
  921.3 15.6 %collective-permute-done.3 = bf16[512,768]{0,1:T(8,128)(2,1)} collective-permute-done((bf16[512,768]{0,1:T(8,128)(2,1)}, bf16[512,768]{0,1:T(8,128)(2,1)}, u32[]{:S(2)}, u32[]{:S(2)}) %collective-permute-start.3) | collective-permute-done | bytes 786464 | tf_op jit(solution)/shard_map/while/body/eval_jaxpr/ppermute | solution.py:15
  939.4 14.4 %collective-permute-done = bf16[512,768]{0,1:T(8,128)(2,1)} collective-permute-done((bf16[512,768]{0,1:T(8,128)(2,1)S(1)}, bf16[512,768]{0,1:T(8,128)(2,1)}, u32[]{:S(2)}, u32[]{:S(2)}) %collective-permute-start) | collective-permute-done | bytes 786464 | tf_op jit(solution)/shard_map/while/body/eval_jaxpr/ppermute | solution.py:15
  953.8 10.6 collective-permute-done.1
  986.2 6.4 bitcast_add_fusion.7
  992.6 9.3 collective-permute-done.2
  1003.2 15.6 %collective-permute-done.3 = bf16[512,768]{0,1:T(8,128)(2,1)} collective-permute-done((bf16[512,768]{0,1:T(8,128)(2,1)}, bf16[512,768]{0,1:T(8,128)(2,1)}, u32[]{:S(2)}, u32[]{:S(2)}) %collective-permute-start.3) | collective-permute-done | bytes 786464 | tf_op jit(solution)/shard_map/while/body/eval_jaxpr/ppermute | solution.py:15
  1021.3 14.4 %collective-permute-done = bf16[512,768]{0,1:T(8,128)(2,1)} collective-permute-done((bf16[512,768]{0,1:T(8,128)(2,1)S(1)}, bf16[512,768]{0,1:T(8,128)(2,1)}, u32[]{:S(2)}, u32[]{:S(2)}) %collective-permute-start) | collective-permute-done | bytes 786464 | tf_op jit(solution)/shard_map/while/body/eval_jaxpr/ppermute | solution.py:15
  1035.7 9.7 collective-permute-done.1
  1067.2 6.4 bitcast_add_fusion.7
  1073.7 9.3 collective-permute-done.2
  1084.3 15.6 %collective-permute-done.3 = bf16[512,768]{0,1:T(8,128)(2,1)} collective-permute-done((bf16[512,768]{0,1:T(8,128)(2,1)}, bf16[512,768]{0,1:T(8,128)(2,1)}, u32[]{:S(2)}, u32[]{:S(2)}) %collective-permute-start.3) | collective-permute-done | bytes 786464 | tf_op jit(solution)/shard_map/while/body/eval_jaxpr/ppermute | solution.py:15
  1102.4 14.4 %collective-permute-done = bf16[512,768]{0,1:T(8,128)(2,1)} collective-permute-done((bf16[512,768]{0,1:T(8,128)(2,1)S(1)}, bf16[512,768]{0,1:T(8,128)(2,1)}, u32[]{:S(2)}, u32[]{:S(2)}) %collective-permute-start) | collective-permute-done | bytes 786464 | tf_op jit(solution)/shard_map/while/body/eval_jaxpr/ppermute | solution.py:15
  1116.8 8.9 collective-permute-done.1
  1138.0 37.4 %reduce-scatter.5.cloned.1.call-done = bf16[192,2304]{1,0:T(8,128)(2,1)} async-done(((bf16[768,2304]{1,0:T(8,128)(2,1)}), bf16[192,2304]{1,0:T(8,128)(2,1)}) %reduce-scatter.5.cloned.1.call-update) | async-done | bytes 884752 | tf_op jit(solution)/shard_map/reduce_scatter | solution.py:272
  1188.3 22.7 %all-reduce.6 = (bf16[192]{0:T(256)(128)(2,1)S(1)}, bf16[192]{0:T(256)(128)(2,1)S(1)}) all-reduce(bf16[192]{0:T(256)(128)(2,1)S(1)} %dynamic-slice.3, bf16[192]{0:T(256)(128)(2,1)S(1)} %dynamic-slice.5), channel_id=1, replica_groups=mesh['ctx'=8,'dp'=4] {'ctx'}, use_global_device_ids=true, to_apply=%region_17.18 | all-reduce | flops 384 | bytes 1536 | tf_op jit(solution)/shard_map/psum | solution.py:286
  1217.6 74.8 %all-reduce.12.cloned.1.call-done = (bf16[192,2304]{1,0:T(8,128)(2,1)}, bf16[192,768]{1,0:T(8,128)(2,1)}, bf16[192,2304]{1,0:T(8,128)(2,1)}, bf16[288,768]{1,0:T(8,128)(2,1)}) async-done(((bf16[192,2304]{1,0:T(8,128)(2,1)}, bf16[192,768]{1,0:T(8,128)(2,1)}, bf16[192,2304]{1,0:T(8,128)(2,1)}, bf16[288,768]{1,0:T(8,128)(2,1)}), (bf16[192,2304]{1,0:T(8,128)(2,1)}, bf16[192,768]{1,0:T(8,128)(2,1)}, ...) | async-done | bytes 2506768 | tf_op jit(solution)/shard_map/psum | solution.py:288
  (465 shorter events, 378.3 us)
Async XLA Ops:
  7.2 13.9 %copy-start.14 = (bf16[1,512,768]{2,1,0:T(8,128)(2,1)S(1)}, bf16[1,512,768]{2,1,0:T(8,128)(2,1)}, u32[]{:S(2)}) copy-start(bf16[1,512,768]{2,1,0:T(8,128)(2,1)} %param.13) | copy-start | bytes 2359300
  7.2 35.9 %all-gather.7.cloned.1.call-start = ((), (), s32[]{:S(2)}) async-start(), calls=%async_computation.4 | async-start | bytes 4423680 | tf_op jit(solution)/shard_map/all_gather | solution.py:88
  7.9 149.1 %all-gather.9.cloned.1.call-start = ((), (), s32[]{:S(2)}) async-start(), calls=%async_computation.5 | async-start | bytes 7077888 | tf_op jit(solution)/shard_map/all_gather | solution.py:131
  20.0 28.8 %copy-start.38 = (f32[768]{0:T(1024)}, f32[768]{0:T(1024)S(1)}, u32[]{:S(2)}) copy-start(f32[768]{0:T(1024)S(1)} %convert_element_type.147) | copy-start | bytes 9220
  21.0 35.0 %copy-start.23 = (f32[512,64]{0,1:T(8,128)}, f32[512,64]{0,1:T(8,128)S(1)}, u32[]{:S(2)}) copy-start(f32[512,64]{0,1:T(8,128)S(1)} %pad_maximum_fusion.4) | copy-start | bytes 393220
  21.0 33.0 %copy-start.28 = (f32[512,64]{0,1:T(8,128)}, f32[512,64]{0,1:T(8,128)S(1)}, u32[]{:S(2)}) copy-start(f32[512,64]{0,1:T(8,128)S(1)} %pad_maximum_fusion.5) | copy-start | bytes 393220
  21.2 27.5 %copy-start.40 = (f32[512]{0:T(512)}, f32[512]{0:T(512)S(1)}, u32[]{:S(2)}) copy-start(f32[512]{0:T(512)S(1)} %broadcast_multiply_fusion.3) | copy-start | bytes 6148
  21.6 27.2 %copy-start.46 = (f32[512]{0:T(512)}, f32[512]{0:T(512)S(1)}, u32[]{:S(2)}) copy-start(f32[512]{0:T(512)S(1)} %fusion.44) | copy-start | bytes 6148
  21.6 27.2 %copy-start.42 = (f32[512]{0:T(512)}, f32[512]{0:T(512)S(1)}, u32[]{:S(2)}) copy-start(f32[512]{0:T(512)S(1)} %fusion.75) | copy-start | bytes 6148
  57.3 199.4 %all-gather.11.cloned.1.call-start = ((), (), s32[]{:S(2)}) async-start(), calls=%async_computation.6 | async-start | bytes 7077888 | tf_op jit(solution)/shard_map/all_gather | solution.py:132
  59.9 355.8 %all-gather.13.cloned.1.call-start = ((), (), s32[]{:S(2)}) async-start(), calls=%async_computation.7 | async-start | bytes 1474560 | tf_op jit(solution)/shard_map/all_gather | solution.py:89
  60.5 359.1 %all-gather.15.cloned.1.call-start = ((), (), s32[]{:S(2)}) async-start(), calls=%async_computation.8 | async-start | bytes 4423680 | tf_op jit(solution)/shard_map/all_gather | solution.py:90
  61.1 365.4 %all-gather.17.cloned.1.call-start = ((), (), s32[]{:S(2)}) async-start(), calls=%async_computation.9 | async-start | bytes 2211840 | tf_op jit(solution)/shard_map/all_gather | solution.py:91
  61.6 1076.3 %reduce-scatter.7.cloned.1.call-start = ((), (), s32[]{:S(2)}) async-start(), calls=%async_computation.11 | async-start | bytes 1474560 | tf_op jit(solution)/shard_map/reduce_scatter | solution.py:275
  276.2 9.6 copy-start.1
  435.8 11.0 copy-start.30
  446.7 691.2 %reduce-scatter.11.cloned.1.call-start = ((), (), s32[]{:S(2)}) async-start(), calls=%async_computation.13 | async-start | bytes 2211840 | tf_op jit(solution)/shard_map/reduce_scatter | solution.py:281
  449.1 688.9 %reduce-scatter.9.cloned.1.call-start = ((), (), s32[]{:S(2)}) async-start(), calls=%async_computation.12 | async-start | bytes 4423680 | tf_op jit(solution)/shard_map/reduce_scatter | solution.py:278
  461.0 714.4 %reduce-scatter.5.cloned.1.call-start = ((), (), s32[]{:S(2)}) async-start(), calls=%async_computation.10 | async-start | bytes 4423680 | tf_op jit(solution)/shard_map/reduce_scatter | solution.py:272
  461.1 664.6 %copy-start.29 = (f32[512,64]{0,1:T(8,128)S(1)}, f32[512,64]{0,1:T(8,128)}, u32[]{:S(2)}) copy-start(f32[512,64]{0,1:T(8,128)} %copy-done.28) | copy-start | bytes 393220
  474.1 23.3 %collective-permute-start.2 = (bf16[512,768]{0,1:T(8,128)(2,1)}, bf16[512,768]{0,1:T(8,128)(2,1)S(1)}, u32[]{:S(2)}, u32[]{:S(2)}) collective-permute-start(bf16[512,768]{0,1:T(8,128)(2,1)} %fusion.151), channel_id=1, source_target_pairs={{0,4},{4,8},{8,12},{12,16},{16,20},{20,24},{24,28},{28,0},{1,5},{5... | collective-permute-start | bytes 2359304 | tf_op jit(solution)/shard_map/while/body/eval_jaxpr/ppermute | solution.py:15
  483.4 31.0 %collective-permute-start.3 = (bf16[512,768]{0,1:T(8,128)(2,1)}, bf16[512,768]{0,1:T(8,128)(2,1)}, u32[]{:S(2)}, u32[]{:S(2)}) collective-permute-start(bf16[512,768]{0,1:T(8,128)(2,1)} %fusion.153), channel_id=1, source_target_pairs={{0,4},{4,8},{8,12},{12,16},{16,20},{20,24},{24,28},{28,0},{1,5},{5... | collective-permute-start | bytes 2359304 | tf_op jit(solution)/shard_map/while/body/eval_jaxpr/ppermute | solution.py:15
  483.4 47.8 %collective-permute-start = (bf16[512,768]{0,1:T(8,128)(2,1)S(1)}, bf16[512,768]{0,1:T(8,128)(2,1)}, u32[]{:S(2)}, u32[]{:S(2)}) collective-permute-start(bf16[512,768]{0,1:T(8,128)(2,1)S(1)} %copy.58), channel_id=1, source_target_pairs={{0,4},{4,8},{8,12},{12,16},{16,20},{20,24},{24,28},{28,0},{1,5},{5... | collective-permute-start | bytes 2359304 | tf_op jit(solution)/shard_map/while/body/eval_jaxpr/ppermute | solution.py:15
  483.4 62.7 %collective-permute-start.1 = (bf16[512,768]{0,1:T(8,128)(2,1)S(1)}, bf16[512,768]{0,1:T(8,128)(2,1)}, u32[]{:S(2)}, u32[]{:S(2)}) collective-permute-start(bf16[512,768]{0,1:T(8,128)(2,1)S(1)} %copy-done.6), channel_id=1, source_target_pairs={{0,4},{4,8},{8,12},{12,16},{16,20},{20,24},{24,28},{28,0},{1,5},{5... | collective-permute-start | bytes 2359304 | tf_op jit(solution)/shard_map/while/body/eval_jaxpr/ppermute | solution.py:15
  498.8 47.3 %copy-start.4 = (bf16[512,12,64]{0,2,1:T(8,128)(2,1)S(1)}, bf16[512,12,64]{0,2,1:T(8,128)(2,1)}, u32[]{:S(2)}) copy-start(bf16[512,12,64]{0,2,1:T(8,128)(2,1)} %copy-done.3) | copy-start | bytes 2359300 | tf_op jit(solution)/shard_map/while
  560.3 23.3 %collective-permute-start.2 = (bf16[512,768]{0,1:T(8,128)(2,1)}, bf16[512,768]{0,1:T(8,128)(2,1)S(1)}, u32[]{:S(2)}, u32[]{:S(2)}) collective-permute-start(bf16[512,768]{0,1:T(8,128)(2,1)} %fusion.151), channel_id=1, source_target_pairs={{0,4},{4,8},{8,12},{12,16},{16,20},{20,24},{24,28},{28,0},{1,5},{5... | collective-permute-start | bytes 2359304 | tf_op jit(solution)/shard_map/while/body/eval_jaxpr/ppermute | solution.py:15
  567.8 32.7 %collective-permute-start.3 = (bf16[512,768]{0,1:T(8,128)(2,1)}, bf16[512,768]{0,1:T(8,128)(2,1)}, u32[]{:S(2)}, u32[]{:S(2)}) collective-permute-start(bf16[512,768]{0,1:T(8,128)(2,1)} %fusion.153), channel_id=1, source_target_pairs={{0,4},{4,8},{8,12},{12,16},{16,20},{20,24},{24,28},{28,0},{1,5},{5... | collective-permute-start | bytes 2359304 | tf_op jit(solution)/shard_map/while/body/eval_jaxpr/ppermute | solution.py:15
  568.8 48.6 %collective-permute-start = (bf16[512,768]{0,1:T(8,128)(2,1)S(1)}, bf16[512,768]{0,1:T(8,128)(2,1)}, u32[]{:S(2)}, u32[]{:S(2)}) collective-permute-start(bf16[512,768]{0,1:T(8,128)(2,1)S(1)} %copy.58), channel_id=1, source_target_pairs={{0,4},{4,8},{8,12},{12,16},{16,20},{20,24},{24,28},{28,0},{1,5},{5... | collective-permute-start | bytes 2359304 | tf_op jit(solution)/shard_map/while/body/eval_jaxpr/ppermute | solution.py:15
  568.9 62.5 %collective-permute-start.1 = (bf16[512,768]{0,1:T(8,128)(2,1)S(1)}, bf16[512,768]{0,1:T(8,128)(2,1)}, u32[]{:S(2)}, u32[]{:S(2)}) collective-permute-start(bf16[512,768]{0,1:T(8,128)(2,1)S(1)} %copy-done.6), channel_id=1, source_target_pairs={{0,4},{4,8},{8,12},{12,16},{16,20},{20,24},{24,28},{28,0},{1,5},{5... | collective-permute-start | bytes 2359304 | tf_op jit(solution)/shard_map/while/body/eval_jaxpr/ppermute | solution.py:15
  585.0 46.5 %copy-start.4 = (bf16[512,12,64]{0,2,1:T(8,128)(2,1)S(1)}, bf16[512,12,64]{0,2,1:T(8,128)(2,1)}, u32[]{:S(2)}) copy-start(bf16[512,12,64]{0,2,1:T(8,128)(2,1)} %copy-done.3) | copy-start | bytes 2359300 | tf_op jit(solution)/shard_map/while
  645.7 23.3 %collective-permute-start.2 = (bf16[512,768]{0,1:T(8,128)(2,1)}, bf16[512,768]{0,1:T(8,128)(2,1)S(1)}, u32[]{:S(2)}, u32[]{:S(2)}) collective-permute-start(bf16[512,768]{0,1:T(8,128)(2,1)} %fusion.151), channel_id=1, source_target_pairs={{0,4},{4,8},{8,12},{12,16},{16,20},{20,24},{24,28},{28,0},{1,5},{5... | collective-permute-start | bytes 2359304 | tf_op jit(solution)/shard_map/while/body/eval_jaxpr/ppermute | solution.py:15
  653.2 32.7 %collective-permute-start.3 = (bf16[512,768]{0,1:T(8,128)(2,1)}, bf16[512,768]{0,1:T(8,128)(2,1)}, u32[]{:S(2)}, u32[]{:S(2)}) collective-permute-start(bf16[512,768]{0,1:T(8,128)(2,1)} %fusion.153), channel_id=1, source_target_pairs={{0,4},{4,8},{8,12},{12,16},{16,20},{20,24},{24,28},{28,0},{1,5},{5... | collective-permute-start | bytes 2359304 | tf_op jit(solution)/shard_map/while/body/eval_jaxpr/ppermute | solution.py:15
  653.7 49.1 %collective-permute-start = (bf16[512,768]{0,1:T(8,128)(2,1)S(1)}, bf16[512,768]{0,1:T(8,128)(2,1)}, u32[]{:S(2)}, u32[]{:S(2)}) collective-permute-start(bf16[512,768]{0,1:T(8,128)(2,1)S(1)} %copy.58), channel_id=1, source_target_pairs={{0,4},{4,8},{8,12},{12,16},{16,20},{20,24},{24,28},{28,0},{1,5},{5... | collective-permute-start | bytes 2359304 | tf_op jit(solution)/shard_map/while/body/eval_jaxpr/ppermute | solution.py:15
  653.8 62.1 %collective-permute-start.1 = (bf16[512,768]{0,1:T(8,128)(2,1)S(1)}, bf16[512,768]{0,1:T(8,128)(2,1)}, u32[]{:S(2)}, u32[]{:S(2)}) collective-permute-start(bf16[512,768]{0,1:T(8,128)(2,1)S(1)} %copy-done.6), channel_id=1, source_target_pairs={{0,4},{4,8},{8,12},{12,16},{16,20},{20,24},{24,28},{28,0},{1,5},{5... | collective-permute-start | bytes 2359304 | tf_op jit(solution)/shard_map/while/body/eval_jaxpr/ppermute | solution.py:15
  670.3 45.6 %copy-start.4 = (bf16[512,12,64]{0,2,1:T(8,128)(2,1)S(1)}, bf16[512,12,64]{0,2,1:T(8,128)(2,1)}, u32[]{:S(2)}) copy-start(bf16[512,12,64]{0,2,1:T(8,128)(2,1)} %copy-done.3) | copy-start | bytes 2359300 | tf_op jit(solution)/shard_map/while
  730.2 23.3 %collective-permute-start.2 = (bf16[512,768]{0,1:T(8,128)(2,1)}, bf16[512,768]{0,1:T(8,128)(2,1)S(1)}, u32[]{:S(2)}, u32[]{:S(2)}) collective-permute-start(bf16[512,768]{0,1:T(8,128)(2,1)} %fusion.151), channel_id=1, source_target_pairs={{0,4},{4,8},{8,12},{12,16},{16,20},{20,24},{24,28},{28,0},{1,5},{5... | collective-permute-start | bytes 2359304 | tf_op jit(solution)/shard_map/while/body/eval_jaxpr/ppermute | solution.py:15
  737.7 32.7 %collective-permute-start.3 = (bf16[512,768]{0,1:T(8,128)(2,1)}, bf16[512,768]{0,1:T(8,128)(2,1)}, u32[]{:S(2)}, u32[]{:S(2)}) collective-permute-start(bf16[512,768]{0,1:T(8,128)(2,1)} %fusion.153), channel_id=1, source_target_pairs={{0,4},{4,8},{8,12},{12,16},{16,20},{20,24},{24,28},{28,0},{1,5},{5... | collective-permute-start | bytes 2359304 | tf_op jit(solution)/shard_map/while/body/eval_jaxpr/ppermute | solution.py:15
  737.8 49.5 %collective-permute-start = (bf16[512,768]{0,1:T(8,128)(2,1)S(1)}, bf16[512,768]{0,1:T(8,128)(2,1)}, u32[]{:S(2)}, u32[]{:S(2)}) collective-permute-start(bf16[512,768]{0,1:T(8,128)(2,1)S(1)} %copy.58), channel_id=1, source_target_pairs={{0,4},{4,8},{8,12},{12,16},{16,20},{20,24},{24,28},{28,0},{1,5},{5... | collective-permute-start | bytes 2359304 | tf_op jit(solution)/shard_map/while/body/eval_jaxpr/ppermute | solution.py:15
  737.9 61.7 %collective-permute-start.1 = (bf16[512,768]{0,1:T(8,128)(2,1)S(1)}, bf16[512,768]{0,1:T(8,128)(2,1)}, u32[]{:S(2)}, u32[]{:S(2)}) collective-permute-start(bf16[512,768]{0,1:T(8,128)(2,1)S(1)} %copy-done.6), channel_id=1, source_target_pairs={{0,4},{4,8},{8,12},{12,16},{16,20},{20,24},{24,28},{28,0},{1,5},{5... | collective-permute-start | bytes 2359304 | tf_op jit(solution)/shard_map/while/body/eval_jaxpr/ppermute | solution.py:15
  754.8 44.7 %copy-start.4 = (bf16[512,12,64]{0,2,1:T(8,128)(2,1)S(1)}, bf16[512,12,64]{0,2,1:T(8,128)(2,1)}, u32[]{:S(2)}) copy-start(bf16[512,12,64]{0,2,1:T(8,128)(2,1)} %copy-done.3) | copy-start | bytes 2359300 | tf_op jit(solution)/shard_map/while
  813.8 23.3 %collective-permute-start.2 = (bf16[512,768]{0,1:T(8,128)(2,1)}, bf16[512,768]{0,1:T(8,128)(2,1)S(1)}, u32[]{:S(2)}, u32[]{:S(2)}) collective-permute-start(bf16[512,768]{0,1:T(8,128)(2,1)} %fusion.151), channel_id=1, source_target_pairs={{0,4},{4,8},{8,12},{12,16},{16,20},{20,24},{24,28},{28,0},{1,5},{5... | collective-permute-start | bytes 2359304 | tf_op jit(solution)/shard_map/while/body/eval_jaxpr/ppermute | solution.py:15
  821.4 32.7 %collective-permute-start.3 = (bf16[512,768]{0,1:T(8,128)(2,1)}, bf16[512,768]{0,1:T(8,128)(2,1)}, u32[]{:S(2)}, u32[]{:S(2)}) collective-permute-start(bf16[512,768]{0,1:T(8,128)(2,1)} %fusion.153), channel_id=1, source_target_pairs={{0,4},{4,8},{8,12},{12,16},{16,20},{20,24},{24,28},{28,0},{1,5},{5... | collective-permute-start | bytes 2359304 | tf_op jit(solution)/shard_map/while/body/eval_jaxpr/ppermute | solution.py:15
  821.4 49.6 %collective-permute-start = (bf16[512,768]{0,1:T(8,128)(2,1)S(1)}, bf16[512,768]{0,1:T(8,128)(2,1)}, u32[]{:S(2)}, u32[]{:S(2)}) collective-permute-start(bf16[512,768]{0,1:T(8,128)(2,1)S(1)} %copy.58), channel_id=1, source_target_pairs={{0,4},{4,8},{8,12},{12,16},{16,20},{20,24},{24,28},{28,0},{1,5},{5... | collective-permute-start | bytes 2359304 | tf_op jit(solution)/shard_map/while/body/eval_jaxpr/ppermute | solution.py:15
  821.4 61.0 %collective-permute-start.1 = (bf16[512,768]{0,1:T(8,128)(2,1)S(1)}, bf16[512,768]{0,1:T(8,128)(2,1)}, u32[]{:S(2)}, u32[]{:S(2)}) collective-permute-start(bf16[512,768]{0,1:T(8,128)(2,1)S(1)} %copy-done.6), channel_id=1, source_target_pairs={{0,4},{4,8},{8,12},{12,16},{16,20},{20,24},{24,28},{28,0},{1,5},{5... | collective-permute-start | bytes 2359304 | tf_op jit(solution)/shard_map/while/body/eval_jaxpr/ppermute | solution.py:15
  838.5 43.9 %copy-start.4 = (bf16[512,12,64]{0,2,1:T(8,128)(2,1)S(1)}, bf16[512,12,64]{0,2,1:T(8,128)(2,1)}, u32[]{:S(2)}) copy-start(bf16[512,12,64]{0,2,1:T(8,128)(2,1)} %copy-done.3) | copy-start | bytes 2359300 | tf_op jit(solution)/shard_map/while
  896.6 23.3 %collective-permute-start.2 = (bf16[512,768]{0,1:T(8,128)(2,1)}, bf16[512,768]{0,1:T(8,128)(2,1)S(1)}, u32[]{:S(2)}, u32[]{:S(2)}) collective-permute-start(bf16[512,768]{0,1:T(8,128)(2,1)} %fusion.151), channel_id=1, source_target_pairs={{0,4},{4,8},{8,12},{12,16},{16,20},{20,24},{24,28},{28,0},{1,5},{5... | collective-permute-start | bytes 2359304 | tf_op jit(solution)/shard_map/while/body/eval_jaxpr/ppermute | solution.py:15
  904.2 32.7 %collective-permute-start.3 = (bf16[512,768]{0,1:T(8,128)(2,1)}, bf16[512,768]{0,1:T(8,128)(2,1)}, u32[]{:S(2)}, u32[]{:S(2)}) collective-permute-start(bf16[512,768]{0,1:T(8,128)(2,1)} %fusion.153), channel_id=1, source_target_pairs={{0,4},{4,8},{8,12},{12,16},{16,20},{20,24},{24,28},{28,0},{1,5},{5... | collective-permute-start | bytes 2359304 | tf_op jit(solution)/shard_map/while/body/eval_jaxpr/ppermute | solution.py:15
  904.2 49.6 %collective-permute-start = (bf16[512,768]{0,1:T(8,128)(2,1)S(1)}, bf16[512,768]{0,1:T(8,128)(2,1)}, u32[]{:S(2)}, u32[]{:S(2)}) collective-permute-start(bf16[512,768]{0,1:T(8,128)(2,1)S(1)} %copy.58), channel_id=1, source_target_pairs={{0,4},{4,8},{8,12},{12,16},{16,20},{20,24},{24,28},{28,0},{1,5},{5... | collective-permute-start | bytes 2359304 | tf_op jit(solution)/shard_map/while/body/eval_jaxpr/ppermute | solution.py:15
  904.2 60.2 %collective-permute-start.1 = (bf16[512,768]{0,1:T(8,128)(2,1)S(1)}, bf16[512,768]{0,1:T(8,128)(2,1)}, u32[]{:S(2)}, u32[]{:S(2)}) collective-permute-start(bf16[512,768]{0,1:T(8,128)(2,1)S(1)} %copy-done.6), channel_id=1, source_target_pairs={{0,4},{4,8},{8,12},{12,16},{16,20},{20,24},{24,28},{28,0},{1,5},{5... | collective-permute-start | bytes 2359304 | tf_op jit(solution)/shard_map/while/body/eval_jaxpr/ppermute | solution.py:15
  921.3 43.0 %copy-start.4 = (bf16[512,12,64]{0,2,1:T(8,128)(2,1)S(1)}, bf16[512,12,64]{0,2,1:T(8,128)(2,1)}, u32[]{:S(2)}) copy-start(bf16[512,12,64]{0,2,1:T(8,128)(2,1)} %copy-done.3) | copy-start | bytes 2359300 | tf_op jit(solution)/shard_map/while
  978.6 23.3 %collective-permute-start.2 = (bf16[512,768]{0,1:T(8,128)(2,1)}, bf16[512,768]{0,1:T(8,128)(2,1)S(1)}, u32[]{:S(2)}, u32[]{:S(2)}) collective-permute-start(bf16[512,768]{0,1:T(8,128)(2,1)} %fusion.151), channel_id=1, source_target_pairs={{0,4},{4,8},{8,12},{12,16},{16,20},{20,24},{24,28},{28,0},{1,5},{5... | collective-permute-start | bytes 2359304 | tf_op jit(solution)/shard_map/while/body/eval_jaxpr/ppermute | solution.py:15
  986.1 32.7 %collective-permute-start.3 = (bf16[512,768]{0,1:T(8,128)(2,1)}, bf16[512,768]{0,1:T(8,128)(2,1)}, u32[]{:S(2)}, u32[]{:S(2)}) collective-permute-start(bf16[512,768]{0,1:T(8,128)(2,1)} %fusion.153), channel_id=1, source_target_pairs={{0,4},{4,8},{8,12},{12,16},{16,20},{20,24},{24,28},{28,0},{1,5},{5... | collective-permute-start | bytes 2359304 | tf_op jit(solution)/shard_map/while/body/eval_jaxpr/ppermute | solution.py:15
  986.1 49.6 %collective-permute-start = (bf16[512,768]{0,1:T(8,128)(2,1)S(1)}, bf16[512,768]{0,1:T(8,128)(2,1)}, u32[]{:S(2)}, u32[]{:S(2)}) collective-permute-start(bf16[512,768]{0,1:T(8,128)(2,1)S(1)} %copy.58), channel_id=1, source_target_pairs={{0,4},{4,8},{8,12},{12,16},{16,20},{20,24},{24,28},{28,0},{1,5},{5... | collective-permute-start | bytes 2359304 | tf_op jit(solution)/shard_map/while/body/eval_jaxpr/ppermute | solution.py:15
  986.1 59.3 %collective-permute-start.1 = (bf16[512,768]{0,1:T(8,128)(2,1)S(1)}, bf16[512,768]{0,1:T(8,128)(2,1)}, u32[]{:S(2)}, u32[]{:S(2)}) collective-permute-start(bf16[512,768]{0,1:T(8,128)(2,1)S(1)} %copy-done.6), channel_id=1, source_target_pairs={{0,4},{4,8},{8,12},{12,16},{16,20},{20,24},{24,28},{28,0},{1,5},{5... | collective-permute-start | bytes 2359304 | tf_op jit(solution)/shard_map/while/body/eval_jaxpr/ppermute | solution.py:15
  1003.2 42.2 %copy-start.4 = (bf16[512,12,64]{0,2,1:T(8,128)(2,1)S(1)}, bf16[512,12,64]{0,2,1:T(8,128)(2,1)}, u32[]{:S(2)}) copy-start(bf16[512,12,64]{0,2,1:T(8,128)(2,1)} %copy-done.3) | copy-start | bytes 2359300 | tf_op jit(solution)/shard_map/while
  1059.6 23.3 %collective-permute-start.2 = (bf16[512,768]{0,1:T(8,128)(2,1)}, bf16[512,768]{0,1:T(8,128)(2,1)S(1)}, u32[]{:S(2)}, u32[]{:S(2)}) collective-permute-start(bf16[512,768]{0,1:T(8,128)(2,1)} %fusion.151), channel_id=1, source_target_pairs={{0,4},{4,8},{8,12},{12,16},{16,20},{20,24},{24,28},{28,0},{1,5},{5... | collective-permute-start | bytes 2359304 | tf_op jit(solution)/shard_map/while/body/eval_jaxpr/ppermute | solution.py:15
  1067.2 32.7 %collective-permute-start.3 = (bf16[512,768]{0,1:T(8,128)(2,1)}, bf16[512,768]{0,1:T(8,128)(2,1)}, u32[]{:S(2)}, u32[]{:S(2)}) collective-permute-start(bf16[512,768]{0,1:T(8,128)(2,1)} %fusion.153), channel_id=1, source_target_pairs={{0,4},{4,8},{8,12},{12,16},{16,20},{20,24},{24,28},{28,0},{1,5},{5... | collective-permute-start | bytes 2359304 | tf_op jit(solution)/shard_map/while/body/eval_jaxpr/ppermute | solution.py:15
  1067.2 49.6 %collective-permute-start = (bf16[512,768]{0,1:T(8,128)(2,1)S(1)}, bf16[512,768]{0,1:T(8,128)(2,1)}, u32[]{:S(2)}, u32[]{:S(2)}) collective-permute-start(bf16[512,768]{0,1:T(8,128)(2,1)S(1)} %copy.58), channel_id=1, source_target_pairs={{0,4},{4,8},{8,12},{12,16},{16,20},{20,24},{24,28},{28,0},{1,5},{5... | collective-permute-start | bytes 2359304 | tf_op jit(solution)/shard_map/while/body/eval_jaxpr/ppermute | solution.py:15
  1067.2 58.4 %collective-permute-start.1 = (bf16[512,768]{0,1:T(8,128)(2,1)S(1)}, bf16[512,768]{0,1:T(8,128)(2,1)}, u32[]{:S(2)}, u32[]{:S(2)}) collective-permute-start(bf16[512,768]{0,1:T(8,128)(2,1)S(1)} %copy-done.6), channel_id=1, source_target_pairs={{0,4},{4,8},{8,12},{12,16},{16,20},{20,24},{24,28},{28,0},{1,5},{5... | collective-permute-start | bytes 2359304 | tf_op jit(solution)/shard_map/while/body/eval_jaxpr/ppermute | solution.py:15
  1084.3 41.3 %copy-start.4 = (bf16[512,12,64]{0,2,1:T(8,128)(2,1)S(1)}, bf16[512,12,64]{0,2,1:T(8,128)(2,1)}, u32[]{:S(2)}) copy-start(bf16[512,12,64]{0,2,1:T(8,128)(2,1)} %copy-done.3) | copy-start | bytes 2359300 | tf_op jit(solution)/shard_map/while
  1137.6 154.8 %all-reduce.12.cloned.1.call-start = ((), (), s32[]{:S(2)}) async-start(), calls=%async_computation.14 | async-start | bytes 5013504 | tf_op jit(solution)/shard_map/psum | solution.py:288
  1180.4 31.7 %copy-start.13 = (f32[512,768]{1,0:T(8,128)S(1)}, f32[512,768]{1,0:T(8,128)}, u32[]{:S(2)}) copy-start(f32[512,768]{1,0:T(8,128)} %copy-done.12) | copy-start | bytes 4718596
  1180.4 31.7 %copy-start.26 = (bf16[1,512,768]{2,1,0:T(8,128)(2,1)S(1)}, bf16[1,512,768]{2,1,0:T(8,128)(2,1)}, u32[]{:S(2)}) copy-start(bf16[1,512,768]{2,1,0:T(8,128)(2,1)} %param.14) | copy-start | bytes 2359300
  1180.4 31.7 %copy-start.45 = (f32[512]{0:T(512)S(1)}, f32[512]{0:T(512)}, u32[]{:S(2)}) copy-start(f32[512]{0:T(512)} %copy-done.44) | copy-start | bytes 6148
  (87 other events, 310.4 us)
Sparse Core Ops, SparseCore 0:
  9.5 33.4 all-gather.6
  57.5 99.4 all-gather.8
  159.0 97.6 all-gather.10
  258.1 15.6 all-gather.12
  275.2 30.7 all-gather.14
  307.4 20.7 all-gather.16
  446.8 23.7 reduce-scatter.6
  473.8 29.1 reduce-scatter.10
  505.6 40.3 reduce-scatter.8
  1137.8 37.5 reduce-scatter.4
  1179.3 113.0 all-reduce.11
where the time goes:
time: 1310 us; the launch traced here: 1300 us
  waiting for transfers between devices  720 us (55%)
  matrix products  312 us (24%)
  local copies, waits for them, and re-layouts  107 us (8%)
  other arithmetic  102 us (8%)
  blocking collectives  36.8 us (3%)
  between operations  16.7 us (1%)
    ppermute x32, waiting for transfers between devices, passed_along(): return lax.ppermute(x, axis, [(i, (i + by) % count) for i in range(count)])  401 us
    all_gather x1, waiting for transfers between devices, body(): lax.all_gather(keys_local, 'ctx', axis=0, tiled=True)  95.1 us
    all_gather x1, waiting for transfers between devices, body(): lax.all_gather(values_local, 'ctx', axis=0, tiled=True)  87.9 us
    psum x1, waiting for transfers between devices, body(): lax.psum(summed[2].astype(jnp.bfloat16), 'ctx').astype(jnp.float32)  74.8 us
    dot_general x8, matrix products, attend(): jnp.einsum('qhd,khd->hqk', queries, key_part, preferred_element_type=jnp....  59.3 us
    while x152, local copies, waits for them, and re-layouts  56.3 us
    dot_general x8, matrix products, attend(): jnp.einsum('hqk,khd->qhd', weights.astype(jnp.bfloat16), value_part, pref...  50.9 us
    dot_general x8, matrix products, backward_block(): jnp.einsum('hqk,khd->qhd', score_grad, key_part, preferred_element_type=j...  50.8 us
  transfers between devices with their start and end apart: 43, of which 37 were waited for; matrix products, arithmetic and copies ran while one was open for 33% of the time, Pallas kernels for 0%

commit v1 on v0

--- a/solution.py
+++ b/solution.py
@@ -285,7 +285,7 @@
     totals = (
         lax.psum(summed[0].astype(jnp.bfloat16), "ctx").astype(jnp.float32),
         lax.psum(summed[1].astype(jnp.bfloat16), "ctx").astype(jnp.float32),
-        lax.psum(summed[2].astype(jnp.bfloat16), "ctx").astype(jnp.float32),
+        jnp.sum(lax.all_gather(summed[2].astype(jnp.bfloat16), "ctx"), axis=0).astype(jnp.float32),
         lax.psum(summed[3].astype(jnp.bfloat16), "ctx").astype(jnp.float32),
         lax.psum(summed[4].astype(jnp.bfloat16), "ctx").astype(jnp.float32),
         lax.psum(summed[5].astype(jnp.bfloat16), "ctx").astype(jnp.float32),

time: 1310 us -> 1400 us (1.069)
  waiting for transfers between devices: 720 us -> 804 us
    all_gather x0 -> x1, waiting for transfers between devices: none -> 105 us  [body(): lax.all_gather(summed[2].astype(jnp.bfloat16), 'ctx')]
    psum x1, waiting for transfers between devices: 74.8 us -> 53.4 us  [body(): lax.psum(summed[3].astype(jnp.bfloat16), 'ctx').astype(jnp.float32)]
    unnamed x99 -> x97, local copies, waits for them, and re-layouts: 41.2 us -> 41.3 us
  transfers between devices with their start and end apart: 43 -> 44, of which waited for: 37 -> 38; matrix products, arithmetic and copies ran while one was open for 33% -> 32% of each run, Pallas kernels for 0% -> 0%
where the time goes in v1:
time: 1400 us; the launch traced here: 1390 us
  waiting for transfers between devices  804 us (57%)
  matrix products  312 us (22%)
  local copies, waits for them, and re-layouts  107 us (8%)
  other arithmetic  106 us (8%)
  blocking collectives  36.1 us (3%)
  between operations  17.1 us (1%)
    ppermute x32, waiting for transfers between devices, passed_along(): return lax.ppermute(x, axis, [(i, (i + by) % count) for i in range(count)])  401 us
    all_gather x1, waiting for transfers between devices, body(): lax.all_gather(summed[2].astype(jnp.bfloat16), 'ctx')  105 us
    all_gather x1, waiting for transfers between devices, body(): lax.all_gather(keys_local, 'ctx', axis=0, tiled=True)  95.1 us
    all_gather x1, waiting for transfers between devices, body(): lax.all_gather(values_local, 'ctx', axis=0, tiled=True)  87.9 us
    dot_general x8, matrix products, attend(): jnp.einsum('qhd,khd->hqk', queries, key_part, preferred_element_type=jnp....  59.4 us
    while x152, local copies, waits for them, and re-layouts  56.4 us
    psum x1, waiting for transfers between devices, body(): lax.psum(summed[3].astype(jnp.bfloat16), 'ctx').astype(jnp.float32)  53.4 us
    dot_general x8, matrix products, attend(): jnp.einsum('hqk,khd->qhd', weights.astype(jnp.bfloat16), value_part, pref...  50.9 us
  transfers between devices with their start and end apart: 44, of which 38 were waited for; matrix products, arithmetic and copies ran while one was open for 32% of the time, Pallas kernels for 0%

profile of v1, /device:TPU:0, one launch (start us, length us, event | category | flops | bytes accessed | tf_op | source)
XLA Modules:
  0.0 1392.8 jit_solution(6642262048987455683)
XLA Ops:
  11.6 8.3 all-reduce.9
  21.6 21.4 %all-gather.9.cloned.1.call-done = bf16[768,2304]{1,0:T(8,128)(2,1)} async-done(((bf16[192,2304]{1,0:T(8,128)(2,1)}), bf16[768,2304]{1,0:T(8,128)(2,1)}) %all-gather.9.cloned.1.call-update) | async-done | bytes 3538960 | tf_op jit(solution)/shard_map/all_gather | solution.py:88
  61.8 95.1 %all-gather.11.cloned.1.call-done = bf16[4096,768]{0,1:T(8,128)(2,1)} async-done(((bf16[512,768]{0,1:T(8,128)(2,1)}), bf16[4096,768]{0,1:T(8,128)(2,1)}) %all-gather.11.cloned.1.call-update) | async-done | bytes 6291472 | tf_op jit(solution)/shard_map/all_gather | solution.py:131
  156.9 7.0 copy.35
  168.8 87.9 %all-gather.13.cloned.1.call-done = bf16[4096,768]{0,1:T(8,128)(2,1)} async-done(((bf16[512,768]{0,1:T(8,128)(2,1)}), bf16[4096,768]{0,1:T(8,128)(2,1)}) %all-gather.13.cloned.1.call-update) | async-done | bytes 6291472 | tf_op jit(solution)/shard_map/all_gather | solution.py:132
  256.6 7.0 copy.36
  268.7 145.6 %while.40 = (s32[]{:T(128)}, f32[12,512]{1,0:T(8,128)S(1)}, f32[12,512]{1,0:T(8,128)S(1)}, f32[512,12,64]{0,2,1:T(8,128)S(1)}, bf16[8,512,12,64]{1,3,2,0:T(8,128...) while((s32[]{:T(128)}, f32[12,512]{1,0:T(8,128)S(1)}, ...), condition=%wide.region_5.6_spmd.clone, body=%wide.region_2.5_spmd.clone.sunk | while | flops 831688704 | bytes 93979776 | solution.py:138
  268.7 7.4 bitcast_reduce_fusion.2
  287.9 7.4 bitcast_reduce_fusion.2
  295.3 6.4 bitcast_add_fusion.6
  306.0 7.4 bitcast_reduce_fusion.2
  313.4 6.7 bitcast_add_fusion.6
  324.4 7.4 bitcast_reduce_fusion.2
  342.4 7.4 bitcast_reduce_fusion.2
  360.4 7.4 bitcast_reduce_fusion.2
  378.4 7.4 bitcast_reduce_fusion.2
  396.3 7.4 bitcast_reduce_fusion.2
  419.5 6.8 fusion.82
  426.4 8.1 fusion.72
  454.5 6.4 convolution_convert_fusion
  461.0 664.6 %while.41 = (s32[]{:T(128)}, bf16[512,768]{0,1:T(8,128)(2,1)}, bf16[512,768]{0,1:T(8,128)(2,1)}, f32[512,768]{0,1:T(8,128)}, f32[512,768]{0,1:T(8,128)}, /*index...) while((s32[]{:T(128)}, bf16[512,768]{0,1:T(8,128)(2,1)}, ...), condition=%wide.region_12.13_spmd.clone, body=%wide.region_11.12_spmd.clone.sunk | while | flops 2043150336 | bytes 191177200 | solution.py:253
  475.6 6.4 fusion.152
  498.7 15.6 %collective-permute-done.3 = bf16[512,768]{0,1:T(8,128)(2,1)} collective-permute-done((bf16[512,768]{0,1:T(8,128)(2,1)}, bf16[512,768]{0,1:T(8,128)(2,1)}, u32[]{:S(2)}, u32[]{:S(2)}) %collective-permute-start.3) | collective-permute-done | bytes 786464 | tf_op jit(solution)/shard_map/while/body/eval_jaxpr/ppermute | solution.py:15
  516.8 14.3 %collective-permute-done = bf16[512,768]{0,1:T(8,128)(2,1)} collective-permute-done((bf16[512,768]{0,1:T(8,128)(2,1)S(1)}, bf16[512,768]{0,1:T(8,128)(2,1)}, u32[]{:S(2)}, u32[]{:S(2)}) %collective-permute-start) | collective-permute-done | bytes 786464 | tf_op jit(solution)/shard_map/while/body/eval_jaxpr/ppermute | solution.py:15
  531.1 14.8 %collective-permute-done.1 = bf16[512,768]{0,1:T(8,128)(2,1)} collective-permute-done((bf16[512,768]{0,1:T(8,128)(2,1)S(1)}, bf16[512,768]{0,1:T(8,128)(2,1)}, u32[]{:S(2)}, u32[]{:S(2)}) %collective-permute-start.1) | collective-permute-done | bytes 786464 | tf_op jit(solution)/shard_map/while/body/eval_jaxpr/ppermute | solution.py:15
  570.7 6.4 bitcast_add_fusion.7
  577.1 6.5 collective-permute-done.2
  584.9 15.6 %collective-permute-done.3 = bf16[512,768]{0,1:T(8,128)(2,1)} collective-permute-done((bf16[512,768]{0,1:T(8,128)(2,1)}, bf16[512,768]{0,1:T(8,128)(2,1)}, u32[]{:S(2)}, u32[]{:S(2)}) %collective-permute-start.3) | collective-permute-done | bytes 786464 | tf_op jit(solution)/shard_map/while/body/eval_jaxpr/ppermute | solution.py:15
  603.0 14.4 %collective-permute-done = bf16[512,768]{0,1:T(8,128)(2,1)} collective-permute-done((bf16[512,768]{0,1:T(8,128)(2,1)S(1)}, bf16[512,768]{0,1:T(8,128)(2,1)}, u32[]{:S(2)}, u32[]{:S(2)}) %collective-permute-start) | collective-permute-done | bytes 786464 | tf_op jit(solution)/shard_map/while/body/eval_jaxpr/ppermute | solution.py:15
  617.4 14.0 %collective-permute-done.1 = bf16[512,768]{0,1:T(8,128)(2,1)} collective-permute-done((bf16[512,768]{0,1:T(8,128)(2,1)S(1)}, bf16[512,768]{0,1:T(8,128)(2,1)}, u32[]{:S(2)}, u32[]{:S(2)}) %collective-permute-start.1) | collective-permute-done | bytes 786464 | tf_op jit(solution)/shard_map/while/body/eval_jaxpr/ppermute | solution.py:15
  654.1 6.4 bitcast_add_fusion.7
  660.5 8.4 collective-permute-done.2
  670.3 15.6 %collective-permute-done.3 = bf16[512,768]{0,1:T(8,128)(2,1)} collective-permute-done((bf16[512,768]{0,1:T(8,128)(2,1)}, bf16[512,768]{0,1:T(8,128)(2,1)}, u32[]{:S(2)}, u32[]{:S(2)}) %collective-permute-start.3) | collective-permute-done | bytes 786464 | tf_op jit(solution)/shard_map/while/body/eval_jaxpr/ppermute | solution.py:15
  688.4 14.4 %collective-permute-done = bf16[512,768]{0,1:T(8,128)(2,1)} collective-permute-done((bf16[512,768]{0,1:T(8,128)(2,1)S(1)}, bf16[512,768]{0,1:T(8,128)(2,1)}, u32[]{:S(2)}, u32[]{:S(2)}) %collective-permute-start) | collective-permute-done | bytes 786464 | tf_op jit(solution)/shard_map/while/body/eval_jaxpr/ppermute | solution.py:15
  702.7 13.1 collective-permute-done.1
  737.9 6.4 bitcast_add_fusion.7
  744.2 9.2 collective-permute-done.2
  754.8 15.6 %collective-permute-done.3 = bf16[512,768]{0,1:T(8,128)(2,1)} collective-permute-done((bf16[512,768]{0,1:T(8,128)(2,1)}, bf16[512,768]{0,1:T(8,128)(2,1)}, u32[]{:S(2)}, u32[]{:S(2)}) %collective-permute-start.3) | collective-permute-done | bytes 786464 | tf_op jit(solution)/shard_map/while/body/eval_jaxpr/ppermute | solution.py:15
  772.9 14.4 %collective-permute-done = bf16[512,768]{0,1:T(8,128)(2,1)} collective-permute-done((bf16[512,768]{0,1:T(8,128)(2,1)S(1)}, bf16[512,768]{0,1:T(8,128)(2,1)}, u32[]{:S(2)}, u32[]{:S(2)}) %collective-permute-start) | collective-permute-done | bytes 786464 | tf_op jit(solution)/shard_map/while/body/eval_jaxpr/ppermute | solution.py:15
  787.2 12.3 collective-permute-done.1
  821.4 6.4 bitcast_add_fusion.7
  827.8 9.3 collective-permute-done.2
  838.4 15.6 %collective-permute-done.3 = bf16[512,768]{0,1:T(8,128)(2,1)} collective-permute-done((bf16[512,768]{0,1:T(8,128)(2,1)}, bf16[512,768]{0,1:T(8,128)(2,1)}, u32[]{:S(2)}, u32[]{:S(2)}) %collective-permute-start.3) | collective-permute-done | bytes 786464 | tf_op jit(solution)/shard_map/while/body/eval_jaxpr/ppermute | solution.py:15
  856.5 14.4 %collective-permute-done = bf16[512,768]{0,1:T(8,128)(2,1)} collective-permute-done((bf16[512,768]{0,1:T(8,128)(2,1)S(1)}, bf16[512,768]{0,1:T(8,128)(2,1)}, u32[]{:S(2)}, u32[]{:S(2)}) %collective-permute-start) | collective-permute-done | bytes 786464 | tf_op jit(solution)/shard_map/while/body/eval_jaxpr/ppermute | solution.py:15
  870.9 11.4 collective-permute-done.1
  904.2 6.4 bitcast_add_fusion.7
  910.6 9.3 collective-permute-done.2
  921.2 15.6 %collective-permute-done.3 = bf16[512,768]{0,1:T(8,128)(2,1)} collective-permute-done((bf16[512,768]{0,1:T(8,128)(2,1)}, bf16[512,768]{0,1:T(8,128)(2,1)}, u32[]{:S(2)}, u32[]{:S(2)}) %collective-permute-start.3) | collective-permute-done | bytes 786464 | tf_op jit(solution)/shard_map/while/body/eval_jaxpr/ppermute | solution.py:15
  939.3 14.4 %collective-permute-done = bf16[512,768]{0,1:T(8,128)(2,1)} collective-permute-done((bf16[512,768]{0,1:T(8,128)(2,1)S(1)}, bf16[512,768]{0,1:T(8,128)(2,1)}, u32[]{:S(2)}, u32[]{:S(2)}) %collective-permute-start) | collective-permute-done | bytes 786464 | tf_op jit(solution)/shard_map/while/body/eval_jaxpr/ppermute | solution.py:15
  953.7 10.6 collective-permute-done.1
  986.1 6.4 bitcast_add_fusion.7
  992.5 9.3 collective-permute-done.2
  1003.2 15.6 %collective-permute-done.3 = bf16[512,768]{0,1:T(8,128)(2,1)} collective-permute-done((bf16[512,768]{0,1:T(8,128)(2,1)}, bf16[512,768]{0,1:T(8,128)(2,1)}, u32[]{:S(2)}, u32[]{:S(2)}) %collective-permute-start.3) | collective-permute-done | bytes 786464 | tf_op jit(solution)/shard_map/while/body/eval_jaxpr/ppermute | solution.py:15
  1021.3 14.4 %collective-permute-done = bf16[512,768]{0,1:T(8,128)(2,1)} collective-permute-done((bf16[512,768]{0,1:T(8,128)(2,1)S(1)}, bf16[512,768]{0,1:T(8,128)(2,1)}, u32[]{:S(2)}, u32[]{:S(2)}) %collective-permute-start) | collective-permute-done | bytes 786464 | tf_op jit(solution)/shard_map/while/body/eval_jaxpr/ppermute | solution.py:15
  1035.6 9.7 collective-permute-done.1
  1067.2 6.4 bitcast_add_fusion.7
  1073.6 9.3 collective-permute-done.2
  1084.3 15.6 %collective-permute-done.3 = bf16[512,768]{0,1:T(8,128)(2,1)} collective-permute-done((bf16[512,768]{0,1:T(8,128)(2,1)}, bf16[512,768]{0,1:T(8,128)(2,1)}, u32[]{:S(2)}, u32[]{:S(2)}) %collective-permute-start.3) | collective-permute-done | bytes 786464 | tf_op jit(solution)/shard_map/while/body/eval_jaxpr/ppermute | solution.py:15
  1102.3 14.4 %collective-permute-done = bf16[512,768]{0,1:T(8,128)(2,1)} collective-permute-done((bf16[512,768]{0,1:T(8,128)(2,1)S(1)}, bf16[512,768]{0,1:T(8,128)(2,1)}, u32[]{:S(2)}, u32[]{:S(2)}) %collective-permute-start) | collective-permute-done | bytes 786464 | tf_op jit(solution)/shard_map/while/body/eval_jaxpr/ppermute | solution.py:15
  1116.7 8.9 collective-permute-done.1
  1138.7 36.9 %reduce-scatter.5.cloned.1.call-done = bf16[192,2304]{1,0:T(8,128)(2,1)} async-done(((bf16[768,2304]{1,0:T(8,128)(2,1)}), bf16[192,2304]{1,0:T(8,128)(2,1)}) %reduce-scatter.5.cloned.1.call-update) | async-done | bytes 884752 | tf_op jit(solution)/shard_map/reduce_scatter | solution.py:272
  1188.4 22.0 %all-reduce.6 = (bf16[192]{0:T(256)(128)(2,1)S(1)}, bf16[192]{0:T(256)(128)(2,1)S(1)}) all-reduce(bf16[192]{0:T(256)(128)(2,1)S(1)} %dynamic-slice.3, bf16[192]{0:T(256)(128)(2,1)S(1)} %dynamic-slice.5), channel_id=1, replica_groups=mesh['ctx'=8,'dp'=4] {'ctx'}, use_global_device_ids=true, to_apply=%region_17.18 | all-reduce | flops 384 | bytes 1536 | tf_op jit(solution)/shard_map/psum | solution.py:286
  1217.0 53.4 %all-reduce.12.cloned.1.call-done = (bf16[192,768]{1,0:T(8,128)(2,1)}, bf16[192,2304]{1,0:T(8,128)(2,1)}, bf16[288,768]{1,0:T(8,128)(2,1)}) async-done(((bf16[192,768]{1,0:T(8,128)(2,1)}, bf16[192,2304]{1,0:T(8,128)(2,1)}, bf16[288,768]{1,0:T(8,128)(2,1)}), (bf16[192,768]{1,0:T(8,128)(2,1)}, bf16[192,2304]{1,0:T(8,128)(2,1)}, bf16[288,768]{1,0:T(8,128)(2,1)})) %all-reduce.12.cloned.1.call-update) | async-done | bytes 1622032 | tf_op jit(solution)/shard_map/psum | solution.py:289
  1274.8 105.2 %all-gather.21.cloned.1.call-done = bf16[1536,2304]{1,0:T(8,128)(2,1)} async-done(((bf16[192,2304]{1,0:T(8,128)(2,1)}), bf16[1536,2304]{1,0:T(8,128)(2,1)}) %all-gather.21.cloned.1.call-update) | async-done | bytes 7077904 | tf_op jit(solution)/shard_map/all_gather | solution.py:288
  (467 shorter events, 389.9 us)
Async XLA Ops:
  7.2 13.9 copy-start.14
  7.2 35.9 %all-gather.9.cloned.1.call-start = ((), (), s32[]{:S(2)}) async-start(), calls=%async_computation.4 | async-start | bytes 4423680 | tf_op jit(solution)/shard_map/all_gather | solution.py:88
  7.9 149.0 %all-gather.11.cloned.1.call-start = ((), (), s32[]{:S(2)}) async-start(), calls=%async_computation.5 | async-start | bytes 7077888 | tf_op jit(solution)/shard_map/all_gather | solution.py:131
  20.0 28.8 %copy-start.37 = (f32[768]{0:T(1024)}, f32[768]{0:T(1024)S(1)}, u32[]{:S(2)}) copy-start(f32[768]{0:T(1024)S(1)} %convert_element_type.149) | copy-start | bytes 9220
  21.0 34.9 %copy-start.23 = (f32[512,64]{0,1:T(8,128)}, f32[512,64]{0,1:T(8,128)S(1)}, u32[]{:S(2)}) copy-start(f32[512,64]{0,1:T(8,128)S(1)} %pad_maximum_fusion.4) | copy-start | bytes 393220
  21.0 32.8 %copy-start.28 = (f32[512,64]{0,1:T(8,128)}, f32[512,64]{0,1:T(8,128)S(1)}, u32[]{:S(2)}) copy-start(f32[512,64]{0,1:T(8,128)S(1)} %pad_maximum_fusion.5) | copy-start | bytes 393220
  21.2 27.6 %copy-start.39 = (f32[512]{0:T(512)}, f32[512]{0:T(512)S(1)}, u32[]{:S(2)}) copy-start(f32[512]{0:T(512)S(1)} %broadcast_multiply_fusion.3) | copy-start | bytes 6148
  21.6 27.2 %copy-start.45 = (f32[512]{0:T(512)}, f32[512]{0:T(512)S(1)}, u32[]{:S(2)}) copy-start(f32[512]{0:T(512)S(1)} %fusion.44) | copy-start | bytes 6148
  21.6 27.2 %copy-start.41 = (f32[512]{0:T(512)}, f32[512]{0:T(512)S(1)}, u32[]{:S(2)}) copy-start(f32[512]{0:T(512)S(1)} %fusion.75) | copy-start | bytes 6148
  57.3 199.4 %all-gather.13.cloned.1.call-start = ((), (), s32[]{:S(2)}) async-start(), calls=%async_computation.6 | async-start | bytes 7077888 | tf_op jit(solution)/shard_map/all_gather | solution.py:132
  59.8 355.8 %all-gather.15.cloned.1.call-start = ((), (), s32[]{:S(2)}) async-start(), calls=%async_computation.7 | async-start | bytes 1474560 | tf_op jit(solution)/shard_map/all_gather | solution.py:89
  60.4 359.2 %all-gather.17.cloned.1.call-start = ((), (), s32[]{:S(2)}) async-start(), calls=%async_computation.8 | async-start | bytes 4423680 | tf_op jit(solution)/shard_map/all_gather | solution.py:90
  61.0 365.4 %all-gather.19.cloned.1.call-start = ((), (), s32[]{:S(2)}) async-start(), calls=%async_computation.9 | async-start | bytes 2211840 | tf_op jit(solution)/shard_map/all_gather | solution.py:91
  61.5 1076.2 %reduce-scatter.7.cloned.1.call-start = ((), (), s32[]{:S(2)}) async-start(), calls=%async_computation.11 | async-start | bytes 1474560 | tf_op jit(solution)/shard_map/reduce_scatter | solution.py:275
  435.7 11.0 copy-start.30
  446.6 691.1 %reduce-scatter.11.cloned.1.call-start = ((), (), s32[]{:S(2)}) async-start(), calls=%async_computation.13 | async-start | bytes 2211840 | tf_op jit(solution)/shard_map/reduce_scatter | solution.py:281
  449.0 688.8 %reduce-scatter.9.cloned.1.call-start = ((), (), s32[]{:S(2)}) async-start(), calls=%async_computation.12 | async-start | bytes 4423680 | tf_op jit(solution)/shard_map/reduce_scatter | solution.py:278
  460.9 714.6 %reduce-scatter.5.cloned.1.call-start = ((), (), s32[]{:S(2)}) async-start(), calls=%async_computation.10 | async-start | bytes 4423680 | tf_op jit(solution)/shard_map/reduce_scatter | solution.py:272
  461.0 664.6 %copy-start.29 = (f32[512,64]{0,1:T(8,128)S(1)}, f32[512,64]{0,1:T(8,128)}, u32[]{:S(2)}) copy-start(f32[512,64]{0,1:T(8,128)} %copy-done.28) | copy-start | bytes 393220
  474.0 23.3 %collective-permute-start.2 = (bf16[512,768]{0,1:T(8,128)(2,1)}, bf16[512,768]{0,1:T(8,128)(2,1)S(1)}, u32[]{:S(2)}, u32[]{:S(2)}) collective-permute-start(bf16[512,768]{0,1:T(8,128)(2,1)} %fusion.151), channel_id=1, source_target_pairs={{0,4},{4,8},{8,12},{12,16},{16,20},{20,24},{24,28},{28,0},{1,5},{5... | collective-permute-start | bytes 2359304 | tf_op jit(solution)/shard_map/while/body/eval_jaxpr/ppermute | solution.py:15
  483.3 31.0 %collective-permute-start.3 = (bf16[512,768]{0,1:T(8,128)(2,1)}, bf16[512,768]{0,1:T(8,128)(2,1)}, u32[]{:S(2)}, u32[]{:S(2)}) collective-permute-start(bf16[512,768]{0,1:T(8,128)(2,1)} %fusion.153), channel_id=1, source_target_pairs={{0,4},{4,8},{8,12},{12,16},{16,20},{20,24},{24,28},{28,0},{1,5},{5... | collective-permute-start | bytes 2359304 | tf_op jit(solution)/shard_map/while/body/eval_jaxpr/ppermute | solution.py:15
  483.3 47.8 %collective-permute-start = (bf16[512,768]{0,1:T(8,128)(2,1)S(1)}, bf16[512,768]{0,1:T(8,128)(2,1)}, u32[]{:S(2)}, u32[]{:S(2)}) collective-permute-start(bf16[512,768]{0,1:T(8,128)(2,1)S(1)} %copy.58), channel_id=1, source_target_pairs={{0,4},{4,8},{8,12},{12,16},{16,20},{20,24},{24,28},{28,0},{1,5},{5... | collective-permute-start | bytes 2359304 | tf_op jit(solution)/shard_map/while/body/eval_jaxpr/ppermute | solution.py:15
  483.3 62.7 %collective-permute-start.1 = (bf16[512,768]{0,1:T(8,128)(2,1)S(1)}, bf16[512,768]{0,1:T(8,128)(2,1)}, u32[]{:S(2)}, u32[]{:S(2)}) collective-permute-start(bf16[512,768]{0,1:T(8,128)(2,1)S(1)} %copy-done.6), channel_id=1, source_target_pairs={{0,4},{4,8},{8,12},{12,16},{16,20},{20,24},{24,28},{28,0},{1,5},{5... | collective-permute-start | bytes 2359304 | tf_op jit(solution)/shard_map/while/body/eval_jaxpr/ppermute | solution.py:15
  498.7 47.3 %copy-start.4 = (bf16[512,12,64]{0,2,1:T(8,128)(2,1)S(1)}, bf16[512,12,64]{0,2,1:T(8,128)(2,1)}, u32[]{:S(2)}) copy-start(bf16[512,12,64]{0,2,1:T(8,128)(2,1)} %copy-done.3) | copy-start | bytes 2359300 | tf_op jit(solution)/shard_map/while
  560.2 23.3 %collective-permute-start.2 = (bf16[512,768]{0,1:T(8,128)(2,1)}, bf16[512,768]{0,1:T(8,128)(2,1)S(1)}, u32[]{:S(2)}, u32[]{:S(2)}) collective-permute-start(bf16[512,768]{0,1:T(8,128)(2,1)} %fusion.151), channel_id=1, source_target_pairs={{0,4},{4,8},{8,12},{12,16},{16,20},{20,24},{24,28},{28,0},{1,5},{5... | collective-permute-start | bytes 2359304 | tf_op jit(solution)/shard_map/while/body/eval_jaxpr/ppermute | solution.py:15
  567.8 32.7 %collective-permute-start.3 = (bf16[512,768]{0,1:T(8,128)(2,1)}, bf16[512,768]{0,1:T(8,128)(2,1)}, u32[]{:S(2)}, u32[]{:S(2)}) collective-permute-start(bf16[512,768]{0,1:T(8,128)(2,1)} %fusion.153), channel_id=1, source_target_pairs={{0,4},{4,8},{8,12},{12,16},{16,20},{20,24},{24,28},{28,0},{1,5},{5... | collective-permute-start | bytes 2359304 | tf_op jit(solution)/shard_map/while/body/eval_jaxpr/ppermute | solution.py:15
  568.8 48.6 %collective-permute-start = (bf16[512,768]{0,1:T(8,128)(2,1)S(1)}, bf16[512,768]{0,1:T(8,128)(2,1)}, u32[]{:S(2)}, u32[]{:S(2)}) collective-permute-start(bf16[512,768]{0,1:T(8,128)(2,1)S(1)} %copy.58), channel_id=1, source_target_pairs={{0,4},{4,8},{8,12},{12,16},{16,20},{20,24},{24,28},{28,0},{1,5},{5... | collective-permute-start | bytes 2359304 | tf_op jit(solution)/shard_map/while/body/eval_jaxpr/ppermute | solution.py:15
  568.9 62.5 %collective-permute-start.1 = (bf16[512,768]{0,1:T(8,128)(2,1)S(1)}, bf16[512,768]{0,1:T(8,128)(2,1)}, u32[]{:S(2)}, u32[]{:S(2)}) collective-permute-start(bf16[512,768]{0,1:T(8,128)(2,1)S(1)} %copy-done.6), channel_id=1, source_target_pairs={{0,4},{4,8},{8,12},{12,16},{16,20},{20,24},{24,28},{28,0},{1,5},{5... | collective-permute-start | bytes 2359304 | tf_op jit(solution)/shard_map/while/body/eval_jaxpr/ppermute | solution.py:15
  584.9 46.5 %copy-start.4 = (bf16[512,12,64]{0,2,1:T(8,128)(2,1)S(1)}, bf16[512,12,64]{0,2,1:T(8,128)(2,1)}, u32[]{:S(2)}) copy-start(bf16[512,12,64]{0,2,1:T(8,128)(2,1)} %copy-done.3) | copy-start | bytes 2359300 | tf_op jit(solution)/shard_map/while
  645.6 23.3 %collective-permute-start.2 = (bf16[512,768]{0,1:T(8,128)(2,1)}, bf16[512,768]{0,1:T(8,128)(2,1)S(1)}, u32[]{:S(2)}, u32[]{:S(2)}) collective-permute-start(bf16[512,768]{0,1:T(8,128)(2,1)} %fusion.151), channel_id=1, source_target_pairs={{0,4},{4,8},{8,12},{12,16},{16,20},{20,24},{24,28},{28,0},{1,5},{5... | collective-permute-start | bytes 2359304 | tf_op jit(solution)/shard_map/while/body/eval_jaxpr/ppermute | solution.py:15
  653.1 32.7 %collective-permute-start.3 = (bf16[512,768]{0,1:T(8,128)(2,1)}, bf16[512,768]{0,1:T(8,128)(2,1)}, u32[]{:S(2)}, u32[]{:S(2)}) collective-permute-start(bf16[512,768]{0,1:T(8,128)(2,1)} %fusion.153), channel_id=1, source_target_pairs={{0,4},{4,8},{8,12},{12,16},{16,20},{20,24},{24,28},{28,0},{1,5},{5... | collective-permute-start | bytes 2359304 | tf_op jit(solution)/shard_map/while/body/eval_jaxpr/ppermute | solution.py:15
  653.7 49.0 %collective-permute-start = (bf16[512,768]{0,1:T(8,128)(2,1)S(1)}, bf16[512,768]{0,1:T(8,128)(2,1)}, u32[]{:S(2)}, u32[]{:S(2)}) collective-permute-start(bf16[512,768]{0,1:T(8,128)(2,1)S(1)} %copy.58), channel_id=1, source_target_pairs={{0,4},{4,8},{8,12},{12,16},{16,20},{20,24},{24,28},{28,0},{1,5},{5... | collective-permute-start | bytes 2359304 | tf_op jit(solution)/shard_map/while/body/eval_jaxpr/ppermute | solution.py:15
  653.8 62.1 %collective-permute-start.1 = (bf16[512,768]{0,1:T(8,128)(2,1)S(1)}, bf16[512,768]{0,1:T(8,128)(2,1)}, u32[]{:S(2)}, u32[]{:S(2)}) collective-permute-start(bf16[512,768]{0,1:T(8,128)(2,1)S(1)} %copy-done.6), channel_id=1, source_target_pairs={{0,4},{4,8},{8,12},{12,16},{16,20},{20,24},{24,28},{28,0},{1,5},{5... | collective-permute-start | bytes 2359304 | tf_op jit(solution)/shard_map/while/body/eval_jaxpr/ppermute | solution.py:15
  670.3 45.6 %copy-start.4 = (bf16[512,12,64]{0,2,1:T(8,128)(2,1)S(1)}, bf16[512,12,64]{0,2,1:T(8,128)(2,1)}, u32[]{:S(2)}) copy-start(bf16[512,12,64]{0,2,1:T(8,128)(2,1)} %copy-done.3) | copy-start | bytes 2359300 | tf_op jit(solution)/shard_map/while
  730.1 23.3 %collective-permute-start.2 = (bf16[512,768]{0,1:T(8,128)(2,1)}, bf16[512,768]{0,1:T(8,128)(2,1)S(1)}, u32[]{:S(2)}, u32[]{:S(2)}) collective-permute-start(bf16[512,768]{0,1:T(8,128)(2,1)} %fusion.151), channel_id=1, source_target_pairs={{0,4},{4,8},{8,12},{12,16},{16,20},{20,24},{24,28},{28,0},{1,5},{5... | collective-permute-start | bytes 2359304 | tf_op jit(solution)/shard_map/while/body/eval_jaxpr/ppermute | solution.py:15
  737.7 32.7 %collective-permute-start.3 = (bf16[512,768]{0,1:T(8,128)(2,1)}, bf16[512,768]{0,1:T(8,128)(2,1)}, u32[]{:S(2)}, u32[]{:S(2)}) collective-permute-start(bf16[512,768]{0,1:T(8,128)(2,1)} %fusion.153), channel_id=1, source_target_pairs={{0,4},{4,8},{8,12},{12,16},{16,20},{20,24},{24,28},{28,0},{1,5},{5... | collective-permute-start | bytes 2359304 | tf_op jit(solution)/shard_map/while/body/eval_jaxpr/ppermute | solution.py:15
  737.7 49.5 %collective-permute-start = (bf16[512,768]{0,1:T(8,128)(2,1)S(1)}, bf16[512,768]{0,1:T(8,128)(2,1)}, u32[]{:S(2)}, u32[]{:S(2)}) collective-permute-start(bf16[512,768]{0,1:T(8,128)(2,1)S(1)} %copy.58), channel_id=1, source_target_pairs={{0,4},{4,8},{8,12},{12,16},{16,20},{20,24},{24,28},{28,0},{1,5},{5... | collective-permute-start | bytes 2359304 | tf_op jit(solution)/shard_map/while/body/eval_jaxpr/ppermute | solution.py:15
  737.8 61.7 %collective-permute-start.1 = (bf16[512,768]{0,1:T(8,128)(2,1)S(1)}, bf16[512,768]{0,1:T(8,128)(2,1)}, u32[]{:S(2)}, u32[]{:S(2)}) collective-permute-start(bf16[512,768]{0,1:T(8,128)(2,1)S(1)} %copy-done.6), channel_id=1, source_target_pairs={{0,4},{4,8},{8,12},{12,16},{16,20},{20,24},{24,28},{28,0},{1,5},{5... | collective-permute-start | bytes 2359304 | tf_op jit(solution)/shard_map/while/body/eval_jaxpr/ppermute | solution.py:15
  754.8 44.7 %copy-start.4 = (bf16[512,12,64]{0,2,1:T(8,128)(2,1)S(1)}, bf16[512,12,64]{0,2,1:T(8,128)(2,1)}, u32[]{:S(2)}) copy-start(bf16[512,12,64]{0,2,1:T(8,128)(2,1)} %copy-done.3) | copy-start | bytes 2359300 | tf_op jit(solution)/shard_map/while
  813.8 23.3 %collective-permute-start.2 = (bf16[512,768]{0,1:T(8,128)(2,1)}, bf16[512,768]{0,1:T(8,128)(2,1)S(1)}, u32[]{:S(2)}, u32[]{:S(2)}) collective-permute-start(bf16[512,768]{0,1:T(8,128)(2,1)} %fusion.151), channel_id=1, source_target_pairs={{0,4},{4,8},{8,12},{12,16},{16,20},{20,24},{24,28},{28,0},{1,5},{5... | collective-permute-start | bytes 2359304 | tf_op jit(solution)/shard_map/while/body/eval_jaxpr/ppermute | solution.py:15
  821.3 32.7 %collective-permute-start.3 = (bf16[512,768]{0,1:T(8,128)(2,1)}, bf16[512,768]{0,1:T(8,128)(2,1)}, u32[]{:S(2)}, u32[]{:S(2)}) collective-permute-start(bf16[512,768]{0,1:T(8,128)(2,1)} %fusion.153), channel_id=1, source_target_pairs={{0,4},{4,8},{8,12},{12,16},{16,20},{20,24},{24,28},{28,0},{1,5},{5... | collective-permute-start | bytes 2359304 | tf_op jit(solution)/shard_map/while/body/eval_jaxpr/ppermute | solution.py:15
  821.3 49.6 %collective-permute-start = (bf16[512,768]{0,1:T(8,128)(2,1)S(1)}, bf16[512,768]{0,1:T(8,128)(2,1)}, u32[]{:S(2)}, u32[]{:S(2)}) collective-permute-start(bf16[512,768]{0,1:T(8,128)(2,1)S(1)} %copy.58), channel_id=1, source_target_pairs={{0,4},{4,8},{8,12},{12,16},{16,20},{20,24},{24,28},{28,0},{1,5},{5... | collective-permute-start | bytes 2359304 | tf_op jit(solution)/shard_map/while/body/eval_jaxpr/ppermute | solution.py:15
  821.3 61.0 %collective-permute-start.1 = (bf16[512,768]{0,1:T(8,128)(2,1)S(1)}, bf16[512,768]{0,1:T(8,128)(2,1)}, u32[]{:S(2)}, u32[]{:S(2)}) collective-permute-start(bf16[512,768]{0,1:T(8,128)(2,1)S(1)} %copy-done.6), channel_id=1, source_target_pairs={{0,4},{4,8},{8,12},{12,16},{16,20},{20,24},{24,28},{28,0},{1,5},{5... | collective-permute-start | bytes 2359304 | tf_op jit(solution)/shard_map/while/body/eval_jaxpr/ppermute | solution.py:15
  838.4 43.9 %copy-start.4 = (bf16[512,12,64]{0,2,1:T(8,128)(2,1)S(1)}, bf16[512,12,64]{0,2,1:T(8,128)(2,1)}, u32[]{:S(2)}) copy-start(bf16[512,12,64]{0,2,1:T(8,128)(2,1)} %copy-done.3) | copy-start | bytes 2359300 | tf_op jit(solution)/shard_map/while
  896.6 23.3 %collective-permute-start.2 = (bf16[512,768]{0,1:T(8,128)(2,1)}, bf16[512,768]{0,1:T(8,128)(2,1)S(1)}, u32[]{:S(2)}, u32[]{:S(2)}) collective-permute-start(bf16[512,768]{0,1:T(8,128)(2,1)} %fusion.151), channel_id=1, source_target_pairs={{0,4},{4,8},{8,12},{12,16},{16,20},{20,24},{24,28},{28,0},{1,5},{5... | collective-permute-start | bytes 2359304 | tf_op jit(solution)/shard_map/while/body/eval_jaxpr/ppermute | solution.py:15
  904.1 32.7 %collective-permute-start.3 = (bf16[512,768]{0,1:T(8,128)(2,1)}, bf16[512,768]{0,1:T(8,128)(2,1)}, u32[]{:S(2)}, u32[]{:S(2)}) collective-permute-start(bf16[512,768]{0,1:T(8,128)(2,1)} %fusion.153), channel_id=1, source_target_pairs={{0,4},{4,8},{8,12},{12,16},{16,20},{20,24},{24,28},{28,0},{1,5},{5... | collective-permute-start | bytes 2359304 | tf_op jit(solution)/shard_map/while/body/eval_jaxpr/ppermute | solution.py:15
  904.1 49.6 %collective-permute-start = (bf16[512,768]{0,1:T(8,128)(2,1)S(1)}, bf16[512,768]{0,1:T(8,128)(2,1)}, u32[]{:S(2)}, u32[]{:S(2)}) collective-permute-start(bf16[512,768]{0,1:T(8,128)(2,1)S(1)} %copy.58), channel_id=1, source_target_pairs={{0,4},{4,8},{8,12},{12,16},{16,20},{20,24},{24,28},{28,0},{1,5},{5... | collective-permute-start | bytes 2359304 | tf_op jit(solution)/shard_map/while/body/eval_jaxpr/ppermute | solution.py:15
  904.1 60.1 %collective-permute-start.1 = (bf16[512,768]{0,1:T(8,128)(2,1)S(1)}, bf16[512,768]{0,1:T(8,128)(2,1)}, u32[]{:S(2)}, u32[]{:S(2)}) collective-permute-start(bf16[512,768]{0,1:T(8,128)(2,1)S(1)} %copy-done.6), channel_id=1, source_target_pairs={{0,4},{4,8},{8,12},{12,16},{16,20},{20,24},{24,28},{28,0},{1,5},{5... | collective-permute-start | bytes 2359304 | tf_op jit(solution)/shard_map/while/body/eval_jaxpr/ppermute | solution.py:15
  921.2 43.0 %copy-start.4 = (bf16[512,12,64]{0,2,1:T(8,128)(2,1)S(1)}, bf16[512,12,64]{0,2,1:T(8,128)(2,1)}, u32[]{:S(2)}) copy-start(bf16[512,12,64]{0,2,1:T(8,128)(2,1)} %copy-done.3) | copy-start | bytes 2359300 | tf_op jit(solution)/shard_map/while
  978.5 23.3 %collective-permute-start.2 = (bf16[512,768]{0,1:T(8,128)(2,1)}, bf16[512,768]{0,1:T(8,128)(2,1)S(1)}, u32[]{:S(2)}, u32[]{:S(2)}) collective-permute-start(bf16[512,768]{0,1:T(8,128)(2,1)} %fusion.151), channel_id=1, source_target_pairs={{0,4},{4,8},{8,12},{12,16},{16,20},{20,24},{24,28},{28,0},{1,5},{5... | collective-permute-start | bytes 2359304 | tf_op jit(solution)/shard_map/while/body/eval_jaxpr/ppermute | solution.py:15
  986.0 32.7 %collective-permute-start.3 = (bf16[512,768]{0,1:T(8,128)(2,1)}, bf16[512,768]{0,1:T(8,128)(2,1)}, u32[]{:S(2)}, u32[]{:S(2)}) collective-permute-start(bf16[512,768]{0,1:T(8,128)(2,1)} %fusion.153), channel_id=1, source_target_pairs={{0,4},{4,8},{8,12},{12,16},{16,20},{20,24},{24,28},{28,0},{1,5},{5... | collective-permute-start | bytes 2359304 | tf_op jit(solution)/shard_map/while/body/eval_jaxpr/ppermute | solution.py:15
  986.0 49.6 %collective-permute-start = (bf16[512,768]{0,1:T(8,128)(2,1)S(1)}, bf16[512,768]{0,1:T(8,128)(2,1)}, u32[]{:S(2)}, u32[]{:S(2)}) collective-permute-start(bf16[512,768]{0,1:T(8,128)(2,1)S(1)} %copy.58), channel_id=1, source_target_pairs={{0,4},{4,8},{8,12},{12,16},{16,20},{20,24},{24,28},{28,0},{1,5},{5... | collective-permute-start | bytes 2359304 | tf_op jit(solution)/shard_map/while/body/eval_jaxpr/ppermute | solution.py:15
  986.1 59.3 %collective-permute-start.1 = (bf16[512,768]{0,1:T(8,128)(2,1)S(1)}, bf16[512,768]{0,1:T(8,128)(2,1)}, u32[]{:S(2)}, u32[]{:S(2)}) collective-permute-start(bf16[512,768]{0,1:T(8,128)(2,1)S(1)} %copy-done.6), channel_id=1, source_target_pairs={{0,4},{4,8},{8,12},{12,16},{16,20},{20,24},{24,28},{28,0},{1,5},{5... | collective-permute-start | bytes 2359304 | tf_op jit(solution)/shard_map/while/body/eval_jaxpr/ppermute | solution.py:15
  1003.2 42.2 %copy-start.4 = (bf16[512,12,64]{0,2,1:T(8,128)(2,1)S(1)}, bf16[512,12,64]{0,2,1:T(8,128)(2,1)}, u32[]{:S(2)}) copy-start(bf16[512,12,64]{0,2,1:T(8,128)(2,1)} %copy-done.3) | copy-start | bytes 2359300 | tf_op jit(solution)/shard_map/while
  1059.6 23.3 %collective-permute-start.2 = (bf16[512,768]{0,1:T(8,128)(2,1)}, bf16[512,768]{0,1:T(8,128)(2,1)S(1)}, u32[]{:S(2)}, u32[]{:S(2)}) collective-permute-start(bf16[512,768]{0,1:T(8,128)(2,1)} %fusion.151), channel_id=1, source_target_pairs={{0,4},{4,8},{8,12},{12,16},{16,20},{20,24},{24,28},{28,0},{1,5},{5... | collective-permute-start | bytes 2359304 | tf_op jit(solution)/shard_map/while/body/eval_jaxpr/ppermute | solution.py:15
  1067.1 32.7 %collective-permute-start.3 = (bf16[512,768]{0,1:T(8,128)(2,1)}, bf16[512,768]{0,1:T(8,128)(2,1)}, u32[]{:S(2)}, u32[]{:S(2)}) collective-permute-start(bf16[512,768]{0,1:T(8,128)(2,1)} %fusion.153), channel_id=1, source_target_pairs={{0,4},{4,8},{8,12},{12,16},{16,20},{20,24},{24,28},{28,0},{1,5},{5... | collective-permute-start | bytes 2359304 | tf_op jit(solution)/shard_map/while/body/eval_jaxpr/ppermute | solution.py:15
  1067.1 49.6 %collective-permute-start = (bf16[512,768]{0,1:T(8,128)(2,1)S(1)}, bf16[512,768]{0,1:T(8,128)(2,1)}, u32[]{:S(2)}, u32[]{:S(2)}) collective-permute-start(bf16[512,768]{0,1:T(8,128)(2,1)S(1)} %copy.58), channel_id=1, source_target_pairs={{0,4},{4,8},{8,12},{12,16},{16,20},{20,24},{24,28},{28,0},{1,5},{5... | collective-permute-start | bytes 2359304 | tf_op jit(solution)/shard_map/while/body/eval_jaxpr/ppermute | solution.py:15
  1067.1 58.4 %collective-permute-start.1 = (bf16[512,768]{0,1:T(8,128)(2,1)S(1)}, bf16[512,768]{0,1:T(8,128)(2,1)}, u32[]{:S(2)}, u32[]{:S(2)}) collective-permute-start(bf16[512,768]{0,1:T(8,128)(2,1)S(1)} %copy-done.6), channel_id=1, source_target_pairs={{0,4},{4,8},{8,12},{12,16},{16,20},{20,24},{24,28},{28,0},{1,5},{5... | collective-permute-start | bytes 2359304 | tf_op jit(solution)/shard_map/while/body/eval_jaxpr/ppermute | solution.py:15
  1084.3 41.3 %copy-start.4 = (bf16[512,12,64]{0,2,1:T(8,128)(2,1)S(1)}, bf16[512,12,64]{0,2,1:T(8,128)(2,1)}, u32[]{:S(2)}) copy-start(bf16[512,12,64]{0,2,1:T(8,128)(2,1)} %copy-done.3) | copy-start | bytes 2359300 | tf_op jit(solution)/shard_map/while
  1137.7 132.7 %all-reduce.12.cloned.1.call-start = ((), (), s32[]{:S(2)}) async-start(), calls=%async_computation.15 | async-start | bytes 3244032 | tf_op jit(solution)/shard_map/psum | solution.py:289
  1138.4 241.6 %all-gather.21.cloned.1.call-start = ((), (), s32[]{:S(2)}) async-start(), calls=%async_computation.14 | async-start | bytes 7962624 | tf_op jit(solution)/shard_map/all_gather | solution.py:288
  1180.5 31.0 %copy-start.13 = (f32[512,768]{1,0:T(8,128)S(1)}, f32[512,768]{1,0:T(8,128)}, u32[]{:S(2)}) copy-start(f32[512,768]{1,0:T(8,128)} %copy-done.12) | copy-start | bytes 4718596
  1180.5 31.0 %copy-start.26 = (bf16[1,512,768]{2,1,0:T(8,128)(2,1)S(1)}, bf16[1,512,768]{2,1,0:T(8,128)(2,1)}, u32[]{:S(2)}) copy-start(bf16[1,512,768]{2,1,0:T(8,128)(2,1)} %param.14) | copy-start | bytes 2359300
  1180.5 31.0 %copy-start.44 = (f32[512]{0:T(512)S(1)}, f32[512]{0:T(512)}, u32[]{:S(2)}) copy-start(f32[512]{0:T(512)} %copy-done.43) | copy-start | bytes 6148
  (87 other events, 320.0 us)
Sparse Core Ops, SparseCore 0:
  9.5 33.4 all-gather.8
  57.4 99.4 all-gather.10
  158.9 97.6 all-gather.12
  258.0 15.6 all-gather.14
  275.1 30.7 all-gather.16
  307.3 20.7 all-gather.18
  446.7 23.7 reduce-scatter.6
  473.7 29.1 reduce-scatter.10
  505.5 40.3 reduce-scatter.8
  1137.8 37.6 reduce-scatter.4
  1179.4 90.9 all-reduce.11
  1272.4 107.5 all-gather.20
